TPU v7x, 512 devices: a whole 4x8x8 slice. The times are simulated.
512 devices in a mesh: fsdp: 32 (over y, z_lo), ex: 16 (over x, z_hi, core).
Axes of the slice: x: 4, y: 8, z: 8 (z_hi: 2, z_lo: 4; z = z_hi * 4 + z_lo), core: 2. Of those that a mesh axis runs over, the one named last changes fastest.
Arguments:
- activations: bfloat16 [65536, 4096], P('ex', 'fsdp'), may hold values from -6 to 6
- out_grads: bfloat16 [65536, 11008], P('ex', 'fsdp'), may hold values from -6 to 6
- in_factor: bfloat16 [4096, 64], P('fsdp'), may hold values from -0.09375 to 0.09375
- out_factor: bfloat16 [11008, 32], P('fsdp'), may hold values from -0.0546875 to 0.0546875
- test_features: float32 [512, 2048], P('fsdp'), may hold values from -6 to 6
Outputs:
- kernel: float32 [2048, 2048], P('fsdp', 'ex')
- scores: float32 [512, 64], P('fsdp', 'ex')
All inputs are finite; a program needn't handle non-finite values.
Results may differ from a plain program's by a relative error of at most 0.0003.
Values sent between devices are 32-bit elements; how exact they have to be, the bound alone decides.
No kernel may reach another device: no remote copies, remote signals or barrier semaphores. Data moves between devices by JAX's collectives and lax.ppermute only.
A program may use at most 64 MiB of HBM per device.

v0:
```python
import math

import jax
import jax.numpy as jnp
from jax import lax
from jax.sharding import PartitionSpec as P

LEN = 1024


def shards(activations, out_grads, in_factor, out_factor, test_features):
    fsdp_count = lax.axis_size("fsdp")
    ex_count = lax.axis_size("ex")
    rows_total = activations.shape[0]
    in_rank = in_factor.shape[1]
    out_rank = out_factor.shape[1]
    feature_width = in_rank * out_rank
    ex_dev = rows_total // LEN
    factor_scale = 1.0 / math.sqrt(LEN)
    own_width = feature_width // fsdp_count
    proj_in = jnp.dot(activations, in_factor, preferred_element_type=jnp.float32)
    proj_out = jnp.dot(out_grads, out_factor, preferred_element_type=jnp.float32)
    combined = lax.psum(jnp.concatenate([proj_in, proj_out], axis=1), "fsdp")
    proj_in = combined[:, :in_rank].reshape(ex_dev, LEN, in_rank)
    proj_out = combined[:, in_rank:].reshape(ex_dev, LEN, out_rank)
    outer_sum = jnp.einsum("etk,etl->ekl", proj_in, proj_out, precision=lax.Precision.HIGHEST)
    phi_all = outer_sum.reshape(ex_dev, feature_width) * factor_scale
    phi_own = lax.dynamic_slice_in_dim(phi_all, lax.axis_index("fsdp") * own_width, own_width, 1)
    scores = jnp.dot(test_features, phi_all.T, precision=lax.Precision.HIGHEST) / math.sqrt(
        feature_width
    )
    col_width = feature_width // ex_count
    col_start = lax.axis_index("ex") * col_width
    row_start = lax.axis_index("fsdp") * own_width
    partial_kernel = jnp.dot(phi_own.T, phi_all, precision=lax.Precision.HIGHEST)
    kernel_tile = lax.psum_scatter(partial_kernel, "ex", scatter_dimension=1, tiled=True)
    row_index = row_start + jnp.arange(own_width, dtype=jnp.int32)[:, None]
    col_index = col_start + jnp.arange(col_width, dtype=jnp.int32)[None, :]
    kernel = kernel_tile / (ex_dev * ex_count) + (row_index == col_index).astype(jnp.float32)
    return (kernel, scores)


def solution(mesh):
    in_specs = (P("ex", "fsdp"), P("ex", "fsdp"), P("fsdp", None), P("fsdp", None), P("fsdp", None))
    out_specs = (P("fsdp", "ex"), P("fsdp", "ex"))
    return jax.shard_map(shards, mesh=mesh, in_specs=in_specs, out_specs=out_specs, check_vma=False)
```

profile of v0, /device:TPU:1, one launch (start us, length us, event | category | flops | bytes accessed | tf_op | source)
XLA Modules:
  0.0 428.8 jit_solution(7843401083871185054)
XLA Ops:
  7.2 0.0 copy-start
  7.2 0.0 copy-start.3
  7.2 0.0 all-reduce.2.cloned.1.call-start
  7.2 1.7 copy-done
  9.0 0.0 copy-start.1
  9.0 1.4 fusion.9
  10.4 0.0 copy-done.3
  10.4 0.0 copy-done.1
  10.4 0.5 fusion.8
  10.9 1.3 pad_maximum_fusion
  12.1 0.0 all-reduce.2.cloned.1.call-update
  12.1 0.0 reduce-scatter.2.cloned.1.call-start
  12.2 299.0 %all-reduce.2.cloned.1.call-done = f32[4096,96]{0,1:T(8,128)} async-done(((f32[4096,96]{0,1:T(8,128)}), f32[4096,96]{0,1:T(8,128)}) %all-reduce.2.cloned.1.call-update) | async-done | bytes 1572880 | tf_op jit(solution)/shard_map/psum | solution.py:23
  311.2 0.0 slice-start
  311.2 0.0 slice-start.1
  311.2 0.0 copy-start.2
  311.2 1.2 slice-done
  312.5 0.1 slice-done.1
  312.6 1.0 convolution_multiply_fusion
  313.6 0.1 copy.11
  313.7 0.1 mul.18
  313.8 1.5 fusion.5
  315.4 0.0 reduce-scatter.2.cloned.1.call-update
  315.4 0.0 copy-done.2
  315.4 0.8 fusion
  316.3 104.3 %reduce-scatter.2.cloned.1.call-done = f32[64,128]{1,0:T(8,128)} async-done(((f32[64,2048]{1,0:T(8,128)}), f32[64,128]{1,0:T(8,128)}) %reduce-scatter.2.cloned.1.call-update) | async-done | bytes 32784 | tf_op jit(solution)/shard_map/reduce_scatter | solution.py:36
  420.5 1.4 convert_add_fusion
  (2 shorter events, 0.0 us)
Async XLA Ops:
  7.2 1.8 copy-start
  7.2 3.2 copy-start.3
  7.2 304.0 %all-reduce.2.cloned.1.call-start = ((), (), s32[]{:S(2)}) async-start(), calls=%async_computation.1 | async-start | bytes 3145728 | tf_op jit(solution)/shard_map/psum | solution.py:23
  9.0 1.4 copy-start.1
  12.1 408.4 %reduce-scatter.2.cloned.1.call-start = ((), (), s32[]{:S(2)}) async-start(), calls=%async_computation.2 | async-start | bytes 557056 | tf_op jit(solution)/shard_map/reduce_scatter | solution.py:36
  311.2 1.2 slice-start
  311.2 1.4 slice-start.1
  311.2 4.2 copy-start.2
Sparse Core Ops, SparseCore 0:
  12.3 298.9 all-reduce.1
  316.5 103.9 reduce-scatter.1
where the time goes:
time: 430 us; the launch traced here: 429 us
  waiting for transfers between devices  403 us (94%)
  between operations  14.1 us (3%)
  matrix products  5.24 us (1%)
    psum x1, waiting for transfers between devices, shards(): combined = lax.psum(jnp.concatenate([proj_in, proj_out], axis=1), 'fsdp')  299 us
    reduce_scatter x1, waiting for transfers between devices, shards(): lax.psum_scatter(partial_kernel, 'ex', scatter_dimension=1, tiled=True)  104 us
  transfers between devices with their start and end apart: 2, of which 2 were waited for; matrix products, arithmetic and copies ran while one was open for 0% of the time, Pallas kernels for 0%

commit v1 on v0

v1 whole, which is shorter than its diff:
```python
import functools
import math

import jax
import jax.numpy as jnp
from jax import lax
from jax.experimental import pallas as pl
from jax.experimental.pallas import tpu as pltpu
from jax.sharding import PartitionSpec as P

LEN = 1024
LANES = 128
HIGHEST = lax.Precision.HIGHEST
VMEM = pl.BlockSpec(memory_space=pltpu.VMEM)


def nt_dot(a, b, **kw):
    return lax.dot_general(a, b, (((1,), (1,)), ((), ())), preferred_element_type=jnp.float32, **kw)


def project_kernel(act_ref, grad_t_ref, in_t_ref, out_t_ref, chunk_ref):
    in_rank = in_t_ref.shape[0]
    proj_in = nt_dot(in_t_ref[...], act_ref[...])
    proj_out = jnp.dot(out_t_ref[...], grad_t_ref[...], preferred_element_type=jnp.float32)
    for s in range(chunk_ref.shape[0]):
        cols = slice(s * LANES, (s + 1) * LANES)
        chunk_ref[s, :in_rank, :] = proj_in[:, cols]
        chunk_ref[s, in_rank:, :] = proj_out[:, cols]


def outer_kernel(in_rank, parts_ref, out_ref, sum_ref):
    total = parts_ref[0]
    for s in range(1, parts_ref.shape[0]):
        total = total + parts_ref[s]
    sum_ref[...] = total
    out_rank = total.shape[0] - in_rank
    per_row = LANES // out_rank
    rows = in_rank // per_row
    proj_in = jnp.concatenate(
        [sum_ref[pl.ds(a, rows, stride=per_row), :] for a in range(per_row)], axis=0
    )
    proj_out = jnp.concatenate([total[in_rank:]] * per_row, axis=0)
    full = nt_dot(proj_in, proj_out, precision=HIGHEST)
    group = lax.broadcasted_iota(jnp.int32, (rows, LANES), 1) // out_rank
    dense = full[:rows]
    for a in range(1, per_row):
        dense = jnp.where(group == a, full[a * rows : (a + 1) * rows], dense)
    out_ref[...] = jnp.broadcast_to(dense[None], out_ref.shape)


def scores_kernel(factor_scale, score_scale, parts_ref, test_ref, send_ref, scores_ref, phi_ref):
    sources, rows, _ = parts_ref.shape
    ex_dev = scores_ref.shape[0]
    slices = sources // ex_dev
    tests = test_ref.shape[0]
    weighted = []
    for x in range(ex_dev):
        phi = parts_ref[x * slices]
        for s in range(1, slices):
            phi = phi + parts_ref[x * slices + s]
        phi = phi * factor_scale
        phi_ref[x * rows : (x + 1) * rows, :] = phi
        acc = jnp.zeros((tests, LANES), jnp.float32)
        for r in range(rows):
            acc = acc + test_ref[:, r * LANES : (r + 1) * LANES] * phi[r : r + 1, :]
        weighted.append(acc)
    ones = jnp.ones((8, LANES), jnp.float32)
    sums = nt_dot(ones, jnp.concatenate(weighted, axis=0), precision=HIGHEST) * score_scale
    for x in range(ex_dev):
        scores_ref[x : x + 1, :] = sums[0:1, x * tests : (x + 1) * tests]
    me = lax.axis_index("fsdp")
    own = phi_ref[pl.ds(me // 2, ex_dev, stride=rows), :]
    own = jnp.where(me % 2 == 0, own, pltpu.roll(own, LANES // 2, 1))
    for r in range(rows):
        send_ref[r, :ex_dev, :] = phi_ref[pl.ds(r, ex_dev, stride=rows), :]
        send_ref[r, ex_dev:, :] = own


def tile_kernel(ex_all, recv_ref, out_ref):
    groups, both, _ = recv_ref.shape
    half = both // 2
    recv = recv_ref[...]
    first = lax.broadcasted_iota(jnp.int32, recv.shape, 1) < half
    cols = jnp.where(first, recv, 0.0).reshape(groups * both, LANES)
    swapped = jnp.concatenate([recv[:, half:], recv[:, :half]], axis=1)
    rows = jnp.where(first, swapped, 0.0).reshape(groups * both, LANES)
    tile = lax.dot_general(
        rows, cols, (((0,), (0,)), ((), ())), preferred_element_type=jnp.float32, precision=HIGHEST
    )
    height = out_ref.shape[0]
    row_start = lax.axis_index("fsdp") * height
    col_start = lax.axis_index("ex") * LANES
    row_index = row_start + lax.broadcasted_iota(jnp.int32, out_ref.shape, 0)
    col_index = col_start + lax.broadcasted_iota(jnp.int32, out_ref.shape, 1)
    eye = jnp.where(row_index == col_index, 1.0, 0.0).astype(jnp.float32)
    out_ref[...] = tile[:height] * (1.0 / ex_all) + eye


def shards(activations, out_grads, in_factor, out_factor, test_features):
    fsdp_count = lax.axis_size("fsdp")
    ex_count = lax.axis_size("ex")
    rows_total, in_width = activations.shape
    out_width = out_grads.shape[1]
    in_rank = in_factor.shape[1]
    out_rank = out_factor.shape[1]
    rank = in_rank + out_rank
    features = in_rank * out_rank
    ex_dev = rows_total // LEN
    tests = test_features.shape[0]
    feature_rows = features // LANES
    steps = 4
    block = rows_total // steps
    f32 = jnp.float32

    chunks = pl.pallas_call(
        project_kernel,
        grid=(steps,),
        in_specs=[
            pl.BlockSpec((block, in_width), lambda i: (i, 0)),
            pl.BlockSpec((out_width, block), lambda i: (0, i)),
            pl.BlockSpec((in_rank, in_width), lambda i: (0, 0)),
            pl.BlockSpec((out_rank, out_width), lambda i: (0, 0)),
        ],
        out_specs=pl.BlockSpec((block // LANES, rank, LANES), lambda i: (i, 0, 0)),
        out_shape=jax.ShapeDtypeStruct((fsdp_count, rank, LANES), f32),
        name="project",
    )(activations, out_grads.T, in_factor.T, out_factor.T)
    parts = lax.all_to_all(chunks, "fsdp", 0, 0, tiled=True)

    outer = pl.pallas_call(
        functools.partial(outer_kernel, in_rank),
        in_specs=[VMEM],
        out_specs=VMEM,
        out_shape=jax.ShapeDtypeStruct((fsdp_count, feature_rows, LANES), f32),
        scratch_shapes=[pltpu.VMEM((rank, LANES), f32)],
        name="outer",
    )(parts)
    partials = lax.all_to_all(outer, "fsdp", 0, 0, tiled=True)

    send, scores_t = pl.pallas_call(
        functools.partial(scores_kernel, 1.0 / math.sqrt(LEN), 1.0 / math.sqrt(features)),
        in_specs=[VMEM, VMEM],
        out_specs=[VMEM, VMEM],
        out_shape=[
            jax.ShapeDtypeStruct((ex_count, 2 * ex_dev, LANES), f32),
            jax.ShapeDtypeStruct((ex_dev, tests), f32),
        ],
        scratch_shapes=[pltpu.VMEM((ex_dev * feature_rows, LANES), f32)],
        name="scores",
    )(partials, test_features)
    recv = lax.all_to_all(send, "ex", 0, 0, tiled=True)

    kernel = pl.pallas_call(
        functools.partial(tile_kernel, ex_dev * ex_count),
        in_specs=[VMEM],
        out_specs=VMEM,
        out_shape=jax.ShapeDtypeStruct((features // fsdp_count, features // ex_count), f32),
        name="tile",
    )(recv)
    return (kernel, scores_t.T)


def solution(mesh):
    in_specs = (P("ex", "fsdp"), P("ex", "fsdp"), P("fsdp", None), P("fsdp", None), P("fsdp", None))
    out_specs = (P("fsdp", "ex"), P("fsdp", "ex"))
    return jax.shard_map(shards, mesh=mesh, in_specs=in_specs, out_specs=out_specs, check_vma=False)
```

time: 430 us -> 104 us (0.24)
  waiting for transfers between devices: 403 us -> 0 us
  blocking collectives: 0 us -> 92.7 us
  between operations: 14.1 us -> 0.63 us
  Pallas kernels: 0 us -> 10.6 us
  matrix products: 5.24 us -> 0 us
    psum x1 -> x0, waiting for transfers between devices: 299 us -> none  [shards(): combined = lax.psum(jnp.concatenate([proj_in, proj_out], axis=1), 'fsdp')]
    reduce_scatter x1 -> x0, waiting for transfers between devices: 104 us -> none  [shards(): lax.psum_scatter(partial_kernel, 'ex', scatter_dimension=1, tiled=True)]
    all_to_all x0 -> x3, blocking collectives: none -> 92.7 us  [the longest x1 52.4 us: shards(): parts = lax.all_to_all(chunks, 'fsdp', 0, 0, tiled=True)]
    pallas_call x0 -> x4, Pallas kernels: none -> 10.6 us  [the longest x1 4.63 us: shards(): pl.pallas_call(project_kernel, grid=(steps,), in_specs=[pl.BlockSpec((blo...]
    dot_general x5 -> x0, matrix products: 5.24 us -> none  [the longest x1 1.51 us: shards(): jnp.dot(phi_own.T, phi_all, precision=lax.Precision.HIGHEST)]
  transfers between devices with their start and end apart: 2 -> 0, of which waited for: 2 -> 0; matrix products, arithmetic and copies ran while one was open for 0% -> 0% of each run, Pallas kernels for 0% -> 0%
where the time goes in v1:
time: 104 us
  blocking collectives  92.7 us (89%)
  Pallas kernels  10.6 us (10%)
    all_to_all x1, blocking collectives, shards(): parts = lax.all_to_all(chunks, 'fsdp', 0, 0, tiled=True)  52.4 us
    all_to_all x1, blocking collectives, shards(): recv = lax.all_to_all(send, 'ex', 0, 0, tiled=True)  23.2 us
    all_to_all x1, blocking collectives, shards(): partials = lax.all_to_all(outer, 'fsdp', 0, 0, tiled=True)  17.1 us
    pallas_call x1, Pallas kernels, shards(): pl.pallas_call(project_kernel, grid=(steps,), in_specs=[pl.BlockSpec((blo...  4.63 us
    pallas_call x1, Pallas kernels, shards(): pl.pallas_call(functools.partial(outer_kernel, in_rank), in_specs=[VMEM],...  2.42 us

profile of v1, /device:TPU:1, one launch (start us, length us, event | category | flops | bytes accessed | tf_op | source)
XLA Modules:
  0.0 104.0 jit_solution(14917936378768212235)
XLA Ops:
  0.6 4.6 %project.1 = f32[32,96,128]{2,1,0:T(8,128)} custom-call(bf16[4096,128]{1,0:T(8,128)(2,1)} %act_ref.1, bf16[344,4096]{1,0:T(8,128)(2,1)} %bitcast.4, bf16[64,128]{1,0:T(8,128)(2,1)} %bitcast.6, bf16[32,344]{1,0:T(8,128)(2,1)} %bitcast.5), custom_call_target="tpu_custom_call" | custom-call | tf_op jit(solution)/shard_map/project/pallas_call | solution.py:115
  5.3 52.4 %all_to_all.15.parts_ref = f32[32,96,128]{2,1,0:T(8,128)} all-to-all(f32[32,96,128]{2,1,0:T(8,128)} %project.1), channel_id=1, replica_groups=mesh['fsdp'=32,'ex'=16] {'fsdp'}, dimensions={0} | all-to-all | bytes 3145728 | tf_op jit(solution)/shard_map/all_to_all | solution.py:128
  57.7 2.4 %outer.1 = f32[32,16,128]{2,1,0:T(8,128)} custom-call(f32[32,96,128]{2,1,0:T(8,128)} %all_to_all.15.parts_ref), custom_call_target="tpu_custom_call" | custom-call | tf_op jit(solution)/shard_map/outer/pallas_call | solution.py:130
  60.1 17.1 %all_to_all.16.parts_ref = f32[32,16,128]{2,1,0:T(8,128)} all-to-all(f32[32,16,128]{2,1,0:T(8,128)} %outer.1), channel_id=1, replica_groups=mesh['fsdp'=32,'ex'=16] {'fsdp'}, dimensions={0} | all-to-all | bytes 524288 | tf_op jit(solution)/shard_map/all_to_all | solution.py:138
  77.2 1.9 %scores.1 = (f32[16,8,128]{2,1,0:T(8,128)}, f32[4,16]{1,0:T(4,128)}) custom-call(f32[32,16,128]{2,1,0:T(8,128)} %all_to_all.16.parts_ref, f32[16,2048]{1,0:T(8,128)} %test_ref.1), custom_call_target="tpu_custom_call" | custom-call | tf_op jit(solution)/shard_map/scores/pallas_call | solution.py:140
  79.0 23.2 %all_to_all.17.recv_ref = f32[16,8,128]{2,1,0:T(8,128)} all-to-all(f32[16,8,128]{2,1,0:T(8,128)} %get-tuple-element.4), channel_id=1, replica_groups=mesh['fsdp'=32,'ex'=16] {'ex'}, dimensions={0} | all-to-all | bytes 131072 | tf_op jit(solution)/shard_map/all_to_all | solution.py:151
  102.3 1.7 %tile.1 = f32[64,128]{1,0:T(8,128)} custom-call(f32[16,8,128]{2,1,0:T(8,128)} %all_to_all.17.recv_ref), custom_call_target="tpu_custom_call" | custom-call | tf_op jit(solution)/shard_map/tile/pallas_call | solution.py:153

commit v2 on v1

--- a/solution.py
+++ b/solution.py
@@ -10,6 +10,8 @@
 
 LEN = 1024
 LANES = 128
+Z = 4
+LIMIT = pltpu.CompilerParams(vmem_limit_bytes=16 * 2**20)
 HIGHEST = lax.Precision.HIGHEST
 VMEM = pl.BlockSpec(memory_space=pltpu.VMEM)
 
@@ -26,6 +28,22 @@
         cols = slice(s * LANES, (s + 1) * LANES)
         chunk_ref[s, :in_rank, :] = proj_in[:, cols]
         chunk_ref[s, in_rank:, :] = proj_out[:, cols]
+
+
+def block_groups(fsdp_count):
+    blocks = range(fsdp_count // Z // 2)
+    place = lambda y, z, dy, dz: (2 * y + dy) * Z + 2 * z + dz
+    pair, halves = range(2), range(Z // 2)
+    near = [[place(y, z, dy, dz) for dy in pair for dz in pair] for y in blocks for z in halves]
+    far = [[place(y, z, dy, dz) for y in blocks for z in halves] for dy in pair for dz in pair]
+    return near, far
+
+
+def sum_kernel(parts_ref, out_ref):
+    total = parts_ref[0]
+    for s in range(1, parts_ref.shape[0]):
+        total = total + parts_ref[s]
+    out_ref[...] = total
 
 
 def outer_kernel(in_rank, parts_ref, out_ref, sum_ref):
@@ -51,14 +69,11 @@
 def scores_kernel(factor_scale, score_scale, parts_ref, test_ref, send_ref, scores_ref, phi_ref):
     sources, rows, _ = parts_ref.shape
     ex_dev = scores_ref.shape[0]
-    slices = sources // ex_dev
+    near = lambda f: f // Z % 2 * 2 + f % 2
     tests = test_ref.shape[0]
     weighted = []
     for x in range(ex_dev):
-        phi = parts_ref[x * slices]
-        for s in range(1, slices):
-            phi = phi + parts_ref[x * slices + s]
-        phi = phi * factor_scale
+        phi = sum(parts_ref[f] for f in range(sources) if near(f) == x) * factor_scale
         phi_ref[x * rows : (x + 1) * rows, :] = phi
         acc = jnp.zeros((tests, LANES), jnp.float32)
         for r in range(rows):
@@ -123,9 +138,20 @@
         ],
         out_specs=pl.BlockSpec((block // LANES, rank, LANES), lambda i: (i, 0, 0)),
         out_shape=jax.ShapeDtypeStruct((fsdp_count, rank, LANES), f32),
+        compiler_params=LIMIT,
         name="project",
     )(activations, out_grads.T, in_factor.T, out_factor.T)
-    parts = lax.all_to_all(chunks, "fsdp", 0, 0, tiled=True)
+    near, far = block_groups(fsdp_count)
+    near_parts = lax.all_to_all(chunks, "fsdp", 0, 0, tiled=True, axis_index_groups=near)
+    near_sum = pl.pallas_call(
+        sum_kernel,
+        in_specs=[VMEM],
+        out_specs=VMEM,
+        out_shape=jax.ShapeDtypeStruct((len(far[0]), rank, LANES), f32),
+        compiler_params=LIMIT,
+        name="near_sum",
+    )(near_parts.reshape(len(near[0]), len(far[0]), rank, LANES))
+    parts = lax.all_to_all(near_sum, "fsdp", 0, 0, tiled=True, axis_index_groups=far)
 
     outer = pl.pallas_call(
         functools.partial(outer_kernel, in_rank),
@@ -133,6 +159,7 @@
         out_specs=VMEM,
         out_shape=jax.ShapeDtypeStruct((fsdp_count, feature_rows, LANES), f32),
         scratch_shapes=[pltpu.VMEM((rank, LANES), f32)],
+        compiler_params=LIMIT,
         name="outer",
     )(parts)
     partials = lax.all_to_all(outer, "fsdp", 0, 0, tiled=True)
@@ -146,6 +173,7 @@
             jax.ShapeDtypeStruct((ex_dev, tests), f32),
         ],
         scratch_shapes=[pltpu.VMEM((ex_dev * feature_rows, LANES), f32)],
+        compiler_params=LIMIT,
         name="scores",
     )(partials, test_features)
     recv = lax.all_to_all(send, "ex", 0, 0, tiled=True)
@@ -155,6 +183,7 @@
         in_specs=[VMEM],
         out_specs=VMEM,
         out_shape=jax.ShapeDtypeStruct((features // fsdp_count, features // ex_count), f32),
+        compiler_params=LIMIT,
         name="tile",
     )(recv)
     return (kernel, scores_t.T)

time: 104 us -> 95.1 us (0.914)
  Pallas kernels: 10.6 us -> 3.59 us
  blocking collectives: 92.7 us -> 86 us
  local copies, waits for them, and re-layouts: 0 us -> 4.47 us
    all_to_all x1 -> x2, blocking collectives: 52.4 us -> 43.3 us  [the longest x1 23.3 us: shards(): lax.all_to_all(near_sum, 'fsdp', 0, 0, tiled=True, axis_index_groups=far)]
    unnamed x0 -> x10, local copies, waits for them, and re-layouts: none -> 4.47 us
    all_to_all x1, blocking collectives: 17.1 us -> 21 us  [shards(): partials = lax.all_to_all(outer, 'fsdp', 0, 0, tiled=True)]
    pallas_call x1, Pallas kernels: 4.63 us -> 1.52 us  [shards(): pl.pallas_call(project_kernel, grid=(steps,), in_specs=[pl.BlockSpec((blo...]
    pallas_call x1, Pallas kernels: 2.42 us -> 0.26 us  [shards(): pl.pallas_call(functools.partial(outer_kernel, in_rank), in_specs=[VMEM],...]
    all_to_all x1, blocking collectives: 23.2 us -> 21.7 us  [shards(): recv = lax.all_to_all(send, 'ex', 0, 0, tiled=True)]
where the time goes in v2:
time: 95.1 us; the launch traced here: 94.7 us
  blocking collectives  86 us (90%)
  local copies, waits for them, and re-layouts  4.47 us (5%)
  Pallas kernels  3.59 us (4%)
    all_to_all x1, blocking collectives, shards(): lax.all_to_all(near_sum, 'fsdp', 0, 0, tiled=True, axis_index_groups=far)  23.3 us
    all_to_all x1, blocking collectives, shards(): recv = lax.all_to_all(send, 'ex', 0, 0, tiled=True)  21.7 us
    all_to_all x1, blocking collectives, shards(): partials = lax.all_to_all(outer, 'fsdp', 0, 0, tiled=True)  21 us
    all_to_all x1, blocking collectives, shards(): lax.all_to_all(chunks, 'fsdp', 0, 0, tiled=True, axis_index_groups=near)  20 us
    unnamed x10, local copies, waits for them, and re-layouts  4.47 us

profile of v2, /device:TPU:1, one launch (start us, length us, event | category | flops | bytes accessed | tf_op | source)
XLA Modules:
  0.0 94.7 jit_solution(17511682114175198144)
XLA Ops:
  0.6 0.0 copy-start
  0.6 1.8 %copy-done = bf16[4096,344]{0,1:T(8,128)(2,1)S(1)} copy-done((bf16[4096,344]{0,1:T(8,128)(2,1)S(1)}, bf16[4096,344]{0,1:T(8,128)(2,1)}, u32[]{:S(2)}) %copy-start) | copy-done | bytes 2818072
  2.4 0.0 copy-start.1
  2.4 1.2 %copy-done.1 = bf16[4096,128]{1,0:T(8,128)(2,1)S(1)} copy-done((bf16[4096,128]{1,0:T(8,128)(2,1)S(1)}, bf16[4096,128]{1,0:T(8,128)(2,1)}, u32[]{:S(2)}) %copy-start.1) | copy-done | bytes 1048600
  3.7 0.0 copy-start.3
  3.7 0.7 copy-done.3
  4.4 0.0 copy-start.4
  4.4 0.7 copy-done.4
  5.1 1.5 %project.1 = f32[32,96,128]{2,1,0:T(8,128)S(1)} custom-call(bf16[4096,128]{1,0:T(8,128)(2,1)S(1)} %copy-done.1, bf16[344,4096]{1,0:T(8,128)(2,1)S(1)} %bitcast.6, bf16[64,128]{1,0:T(8,128)(2,1)S(1)} %bitcast.8, bf16[32,344]{1,0:T(8,128)(2,1)S(1)} %bitcast.7), custom_call_target="tpu_custom_call" | custom-call | tf_op jit(solution)/shard_map/project/pallas_call | solution.py:130
  6.6 20.0 %all_to_all.20 = f32[32,96,128]{2,1,0:T(8,128)S(1)} all-to-all(f32[32,96,128]{2,1,0:T(8,128)S(1)} %project.1), channel_id=1, replica_groups={{0,16,64,80},{32,48,96,112},{128,144,192,208},{160,176,224,240},{256,27..., dimensions={0} | all-to-all | bytes 3145728 | tf_op jit(solution)/shard_map/all_to_all | solution.py:145
  26.6 0.0 copy-start.2
  26.6 0.1 near_sum.1
  26.7 23.3 %all_to_all.21.parts_ref = f32[8,96,128]{2,1,0:T(8,128)S(1)} all-to-all(f32[8,96,128]{2,1,0:T(8,128)S(1)} %near_sum.1), channel_id=1, replica_groups={{0,32,128,160,256,288,384,416},{16,48,144,176,272,304,400,432},{64,96,1..., dimensions={0} | all-to-all | bytes 786432 | tf_op jit(solution)/shard_map/all_to_all | solution.py:154
  50.0 0.3 outer.1
  50.3 21.0 %all_to_all.22.parts_ref = f32[32,16,128]{2,1,0:T(8,128)S(1)} all-to-all(f32[32,16,128]{2,1,0:T(8,128)S(1)} %outer.1), channel_id=1, replica_groups=mesh['fsdp'=32,'ex'=16] {'fsdp'}, dimensions={0} | all-to-all | bytes 524288 | tf_op jit(solution)/shard_map/all_to_all | solution.py:165
  71.2 0.0 copy-done.2
  71.2 0.9 scores.1
  72.1 21.7 %all_to_all.23.recv_ref = f32[16,8,128]{2,1,0:T(8,128)S(1)} all-to-all(f32[16,8,128]{2,1,0:T(8,128)S(1)} %get-tuple-element.4), channel_id=1, replica_groups=mesh['fsdp'=32,'ex'=16] {'ex'}, dimensions={0} | all-to-all | bytes 131072 | tf_op jit(solution)/shard_map/all_to_all | solution.py:179
  93.8 0.9 tile.1
Async XLA Ops:
  0.6 1.8 %copy-start = (bf16[4096,344]{0,1:T(8,128)(2,1)S(1)}, bf16[4096,344]{0,1:T(8,128)(2,1)}, u32[]{:S(2)}) copy-start(bf16[4096,344]{0,1:T(8,128)(2,1)} %param.6) | copy-start | bytes 8454148
  2.4 1.2 %copy-start.1 = (bf16[4096,128]{1,0:T(8,128)(2,1)S(1)}, bf16[4096,128]{1,0:T(8,128)(2,1)}, u32[]{:S(2)}) copy-start(bf16[4096,128]{1,0:T(8,128)(2,1)} %act_ref.1) | copy-start | bytes 3145732
  3.7 0.7 copy-start.3
  4.4 0.7 copy-start.4
  26.6 44.6 %copy-start.2 = (f32[16,2048]{1,0:T(8,128)S(1)}, f32[16,2048]{1,0:T(8,128)}, u32[]{:S(2)}) copy-start(f32[16,2048]{1,0:T(8,128)} %test_ref.1) | copy-start | bytes 393220

commit v3 on v2

--- a/solution.py
+++ b/solution.py
@@ -14,20 +14,47 @@
 LIMIT = pltpu.CompilerParams(vmem_limit_bytes=16 * 2**20)
 HIGHEST = lax.Precision.HIGHEST
 VMEM = pl.BlockSpec(memory_space=pltpu.VMEM)
+HBM = pl.BlockSpec(memory_space=pltpu.HBM)
 
 
 def nt_dot(a, b, **kw):
     return lax.dot_general(a, b, (((1,), (1,)), ((), ())), preferred_element_type=jnp.float32, **kw)
 
 
-def project_kernel(act_ref, grad_t_ref, in_t_ref, out_t_ref, chunk_ref):
-    in_rank = in_t_ref.shape[0]
-    proj_in = nt_dot(in_t_ref[...], act_ref[...])
-    proj_out = jnp.dot(out_t_ref[...], grad_t_ref[...], preferred_element_type=jnp.float32)
-    for s in range(chunk_ref.shape[0]):
-        cols = slice(s * LANES, (s + 1) * LANES)
-        chunk_ref[s, :in_rank, :] = proj_in[:, cols]
-        chunk_ref[s, in_rank:, :] = proj_out[:, cols]
+def project_kernel(act_hbm, grad_t_hbm, in_t_hbm, out_t_hbm, chunk_hbm, act, grad_t, in_t, out_t, chunk, sems, out_sems):
+    steps, block, _ = act.shape
+    in_rank = in_t.shape[0]
+    slices = block // LANES
+    weights = [
+        pltpu.make_async_copy(in_t_hbm, in_t, sems.at[0]),
+        pltpu.make_async_copy(out_t_hbm, out_t, sems.at[1]),
+    ]
+    acts, grads, outs = [], [], []
+    for i in range(steps):
+        rows = pl.ds(i * block, block)
+        own = pl.ds(i * slices, slices)
+        acts.append(pltpu.make_async_copy(act_hbm.at[rows, :], act.at[i], sems.at[2 + 2 * i]))
+        grads.append(pltpu.make_async_copy(grad_t_hbm.at[:, rows], grad_t.at[i], sems.at[3 + 2 * i]))
+        outs.append(pltpu.make_async_copy(chunk.at[own], chunk_hbm.at[own], out_sems.at[i]))
+    for copy in weights:
+        copy.start()
+    for i in range(steps):
+        acts[i].start()
+        grads[i].start()
+    for copy in weights:
+        copy.wait()
+    for i in range(steps):
+        acts[i].wait()
+        proj_in = nt_dot(in_t[...], act[i])
+        grads[i].wait()
+        proj_out = jnp.dot(out_t[...], grad_t[i], preferred_element_type=jnp.float32)
+        for s in range(slices):
+            cols = slice(s * LANES, (s + 1) * LANES)
+            chunk[i * slices + s, :in_rank, :] = proj_in[:, cols]
+            chunk[i * slices + s, in_rank:, :] = proj_out[:, cols]
+        outs[i].start()
+    for copy in outs:
+        copy.wait()
 
 
 def block_groups(fsdp_count):
@@ -123,22 +150,26 @@
     ex_dev = rows_total // LEN
     tests = test_features.shape[0]
     feature_rows = features // LANES
-    steps = 4
+    steps = 2
     block = rows_total // steps
     f32 = jnp.float32
 
+    bf16 = activations.dtype
     chunks = pl.pallas_call(
         project_kernel,
-        grid=(steps,),
-        in_specs=[
-            pl.BlockSpec((block, in_width), lambda i: (i, 0)),
-            pl.BlockSpec((out_width, block), lambda i: (0, i)),
-            pl.BlockSpec((in_rank, in_width), lambda i: (0, 0)),
-            pl.BlockSpec((out_rank, out_width), lambda i: (0, 0)),
+        in_specs=[HBM] * 4,
+        out_specs=HBM,
+        out_shape=jax.ShapeDtypeStruct((fsdp_count, rank, LANES), f32),
+        scratch_shapes=[
+            pltpu.VMEM((steps, block, in_width), bf16),
+            pltpu.VMEM((steps, out_width, block), bf16),
+            pltpu.VMEM((in_rank, in_width), bf16),
+            pltpu.VMEM((out_rank, out_width), bf16),
+            pltpu.VMEM((fsdp_count, rank, LANES), f32),
+            pltpu.SemaphoreType.DMA((2 + 2 * steps,)),
+            pltpu.SemaphoreType.DMA((steps,)),
         ],
-        out_specs=pl.BlockSpec((block // LANES, rank, LANES), lambda i: (i, 0, 0)),
-        out_shape=jax.ShapeDtypeStruct((fsdp_count, rank, LANES), f32),
-        compiler_params=LIMIT,
+        compiler_params=pltpu.CompilerParams(vmem_limit_bytes=58 * 2**20),
         name="project",
     )(activations, out_grads.T, in_factor.T, out_factor.T)
     near, far = block_groups(fsdp_count)

time: 95.1 us -> 93.9 us (0.987)
  local copies, waits for them, and re-layouts: 4.47 us -> 0.01 us
  Pallas kernels: 3.59 us -> 5.65 us
  blocking collectives: 86 us -> 87.3 us
    unnamed x10 -> x2, local copies, waits for them, and re-layouts: 4.47 us -> 0.01 us
    pallas_call x1, Pallas kernels: 1.52 us -> 3.58 us  [shards(): pl.pallas_call(project_kernel, in_specs=[HBM] * 4, out_specs=HBM, out_sha...]
    all_to_all x1, blocking collectives: 23.3 us -> 25.2 us  [shards(): lax.all_to_all(near_sum, 'fsdp', 0, 0, tiled=True, axis_index_groups=far)]
where the time goes in v3:
time: 93.9 us; the launch traced here: 93.6 us
  blocking collectives  87.3 us (93%)
  Pallas kernels  5.65 us (6%)
    all_to_all x1, blocking collectives, shards(): lax.all_to_all(near_sum, 'fsdp', 0, 0, tiled=True, axis_index_groups=far)  25.2 us
    all_to_all x1, blocking collectives, shards(): recv = lax.all_to_all(send, 'ex', 0, 0, tiled=True)  22.5 us
    all_to_all x1, blocking collectives, shards(): partials = lax.all_to_all(outer, 'fsdp', 0, 0, tiled=True)  20.2 us
    all_to_all x1, blocking collectives, shards(): lax.all_to_all(chunks, 'fsdp', 0, 0, tiled=True, axis_index_groups=near)  19.4 us
    pallas_call x1, Pallas kernels, shards(): pl.pallas_call(project_kernel, in_specs=[HBM] * 4, out_specs=HBM, out_sha...  3.58 us

profile of v3, /device:TPU:1, one launch (start us, length us, event | category | flops | bytes accessed | tf_op | source)
XLA Modules:
  0.0 93.6 jit_solution(9502510572916404520)
XLA Ops:
  0.6 3.6 %project.1 = f32[32,96,128]{2,1,0:T(8,128)} custom-call(bf16[4096,128]{1,0:T(8,128)(2,1)} %act_hbm.1, bf16[344,4096]{1,0:T(8,128)(2,1)} %bitcast.6, bf16[64,128]{1,0:T(8,128)(2,1)} %bitcast.8, bf16[32,344]{1,0:T(8,128)(2,1)} %bitcast.7), custom_call_target="tpu_custom_call" | custom-call | tf_op jit(solution)/shard_map/project/pallas_call | solution.py:158
  4.2 19.4 %all_to_all.20 = f32[32,96,128]{2,1,0:T(8,128)S(1)} all-to-all(f32[32,96,128]{2,1,0:T(8,128)} %project.1), channel_id=1, replica_groups={{0,16,64,80},{32,48,96,112},{128,144,192,208},{160,176,224,240},{256,27..., dimensions={0} | all-to-all | bytes 3145728 | tf_op jit(solution)/shard_map/all_to_all | solution.py:176
  23.7 0.0 copy-start
  23.7 0.1 near_sum.1
  23.7 25.2 %all_to_all.21.parts_ref = f32[8,96,128]{2,1,0:T(8,128)S(1)} all-to-all(f32[8,96,128]{2,1,0:T(8,128)S(1)} %near_sum.1), channel_id=1, replica_groups={{0,32,128,160,256,288,384,416},{16,48,144,176,272,304,400,432},{64,96,1..., dimensions={0} | all-to-all | bytes 786432 | tf_op jit(solution)/shard_map/all_to_all | solution.py:185
  48.9 0.3 outer.1
  49.2 20.2 %all_to_all.22.parts_ref = f32[32,16,128]{2,1,0:T(8,128)S(1)} all-to-all(f32[32,16,128]{2,1,0:T(8,128)S(1)} %outer.1), channel_id=1, replica_groups=mesh['fsdp'=32,'ex'=16] {'fsdp'}, dimensions={0} | all-to-all | bytes 524288 | tf_op jit(solution)/shard_map/all_to_all | solution.py:196
  69.4 0.0 copy-done
  69.4 0.9 scores.1
  70.3 22.5 %all_to_all.23.recv_ref = f32[16,8,128]{2,1,0:T(8,128)S(1)} all-to-all(f32[16,8,128]{2,1,0:T(8,128)S(1)} %get-tuple-element.4), channel_id=1, replica_groups=mesh['fsdp'=32,'ex'=16] {'ex'}, dimensions={0} | all-to-all | bytes 131072 | tf_op jit(solution)/shard_map/all_to_all | solution.py:210
  92.8 0.9 tile.1
Async XLA Ops:
  23.7 45.8 %copy-start = (f32[16,2048]{1,0:T(8,128)S(1)}, f32[16,2048]{1,0:T(8,128)}, u32[]{:S(2)}) copy-start(f32[16,2048]{1,0:T(8,128)} %test_ref.1) | copy-start | bytes 393220

commit v4 on v2

--- a/solution.py
+++ b/solution.py
@@ -20,14 +20,26 @@
     return lax.dot_general(a, b, (((1,), (1,)), ((), ())), preferred_element_type=jnp.float32, **kw)
 
 
-def project_kernel(act_ref, grad_t_ref, in_t_ref, out_t_ref, chunk_ref):
-    in_rank = in_t_ref.shape[0]
-    proj_in = nt_dot(in_t_ref[...], act_ref[...])
-    proj_out = jnp.dot(out_t_ref[...], grad_t_ref[...], preferred_element_type=jnp.float32)
-    for s in range(chunk_ref.shape[0]):
-        cols = slice(s * LANES, (s + 1) * LANES)
-        chunk_ref[s, :in_rank, :] = proj_in[:, cols]
-        chunk_ref[s, in_rank:, :] = proj_out[:, cols]
+def block_place(f):
+    return f // Z % 2 * 2 + f % 2
+
+
+def place_order(ex_count):
+    own = block_place(lax.axis_index("fsdp"))
+    first = 2 - lax.axis_index("ex") % 2
+    return own ^ first, own ^ 3, own, own ^ 3 ^ first
+
+
+def project_kernel(along_rows, ex_count, arg_ref, weights_ref, give_ref, keep_ref):
+    for k, place in enumerate(place_order(ex_count)):
+        own = pl.ds(pl.multiple_of(place * LEN, LEN), LEN)
+        if along_rows:
+            proj = nt_dot(weights_ref[...], arg_ref[own, :])
+        else:
+            proj = jnp.dot(weights_ref[...], arg_ref[:, own], preferred_element_type=jnp.float32)
+        out_ref = keep_ref if k >= 2 else give_ref
+        for s in range(LEN // LANES):
+            out_ref[k % 2, s] = proj[:, s * LANES : (s + 1) * LANES]
 
 
 def block_groups(fsdp_count):
@@ -39,11 +51,15 @@
     return near, far
 
 
-def sum_kernel(parts_ref, out_ref):
-    total = parts_ref[0]
-    for s in range(1, parts_ref.shape[0]):
-        total = total + parts_ref[s]
-    out_ref[...] = total
+def pair_sum_kernel(keep_ref, recv_ref, keep_next_ref, give_next_ref):
+    keep_next_ref[...] = keep_ref[0] + recv_ref[0]
+    give_next_ref[...] = keep_ref[1] + recv_ref[1]
+
+
+def near_sum_kernel(keep_in_ref, recv_in_ref, keep_out_ref, recv_out_ref, sum_ref):
+    in_rank = keep_in_ref.shape[1]
+    sum_ref[:, :in_rank, :] = keep_in_ref[...] + recv_in_ref[...]
+    sum_ref[:, in_rank:, :] = keep_out_ref[...] + recv_out_ref[...]
 
 
 def outer_kernel(in_rank, parts_ref, out_ref, sum_ref):
@@ -66,15 +82,25 @@
     out_ref[...] = jnp.broadcast_to(dense[None], out_ref.shape)
 
 
-def scores_kernel(factor_scale, score_scale, parts_ref, test_ref, send_ref, scores_ref, phi_ref):
+def features_kernel(factor_scale, ex_dev, parts_ref, phi_ref, send_ref):
     sources, rows, _ = parts_ref.shape
-    ex_dev = scores_ref.shape[0]
-    near = lambda f: f // Z % 2 * 2 + f % 2
-    tests = test_ref.shape[0]
+    for x in range(ex_dev):
+        phi = sum(parts_ref[f] for f in range(sources) if block_place(f) == x) * factor_scale
+        phi_ref[x * rows : (x + 1) * rows, :] = phi
+    me = lax.axis_index("fsdp")
+    own = phi_ref[pl.ds(me // 2, ex_dev, stride=rows), :]
+    own = jnp.where(me % 2 == 0, own, pltpu.roll(own, LANES // 2, 1))
+    for r in range(rows):
+        send_ref[r, :ex_dev, :] = phi_ref[pl.ds(r, ex_dev, stride=rows), :]
+        send_ref[r, ex_dev:, :] = own
+
+
+def scores_kernel(score_scale, phi_ref, test_ref, scores_ref):
+    ex_dev, tests = scores_ref.shape
+    rows = phi_ref.shape[0] // ex_dev
     weighted = []
     for x in range(ex_dev):
-        phi = sum(parts_ref[f] for f in range(sources) if near(f) == x) * factor_scale
-        phi_ref[x * rows : (x + 1) * rows, :] = phi
+        phi = phi_ref[x * rows : (x + 1) * rows, :]
         acc = jnp.zeros((tests, LANES), jnp.float32)
         for r in range(rows):
             acc = acc + test_ref[:, r * LANES : (r + 1) * LANES] * phi[r : r + 1, :]
@@ -83,12 +109,6 @@
     sums = nt_dot(ones, jnp.concatenate(weighted, axis=0), precision=HIGHEST) * score_scale
     for x in range(ex_dev):
         scores_ref[x : x + 1, :] = sums[0:1, x * tests : (x + 1) * tests]
-    me = lax.axis_index("fsdp")
-    own = phi_ref[pl.ds(me // 2, ex_dev, stride=rows), :]
-    own = jnp.where(me % 2 == 0, own, pltpu.roll(own, LANES // 2, 1))
-    for r in range(rows):
-        send_ref[r, :ex_dev, :] = phi_ref[pl.ds(r, ex_dev, stride=rows), :]
-        send_ref[r, ex_dev:, :] = own
 
 
 def tile_kernel(ex_all, recv_ref, out_ref):
@@ -123,34 +143,57 @@
     ex_dev = rows_total // LEN
     tests = test_features.shape[0]
     feature_rows = features // LANES
-    steps = 4
-    block = rows_total // steps
     f32 = jnp.float32
-
-    chunks = pl.pallas_call(
-        project_kernel,
-        grid=(steps,),
-        in_specs=[
-            pl.BlockSpec((block, in_width), lambda i: (i, 0)),
-            pl.BlockSpec((out_width, block), lambda i: (0, i)),
-            pl.BlockSpec((in_rank, in_width), lambda i: (0, 0)),
-            pl.BlockSpec((out_rank, out_width), lambda i: (0, 0)),
-        ],
-        out_specs=pl.BlockSpec((block // LANES, rank, LANES), lambda i: (i, 0, 0)),
-        out_shape=jax.ShapeDtypeStruct((fsdp_count, rank, LANES), f32),
-        compiler_params=LIMIT,
-        name="project",
-    )(activations, out_grads.T, in_factor.T, out_factor.T)
     near, far = block_groups(fsdp_count)
-    near_parts = lax.all_to_all(chunks, "fsdp", 0, 0, tiled=True, axis_index_groups=near)
+    slices = len(far[0])
+
+    def swap(value, step):
+        pairs = []
+        for e in range(ex_count):
+            mask = 2 - e % 2 if step == 0 else 1 + e % 2
+            for group in near:
+                pairs += [(f * ex_count + e, group[b ^ mask] * ex_count + e) for b, f in enumerate(group)]
+        return lax.ppermute(value, ("fsdp", "ex"), pairs)
+
+    def project(arg, weights, along_rows, name):
+        out_shape = jax.ShapeDtypeStruct((2, slices, weights.shape[0], LANES), f32)
+        return pl.pallas_call(
+            functools.partial(project_kernel, along_rows, ex_count),
+            in_specs=[VMEM] * 2,
+            out_specs=[VMEM] * 2,
+            out_shape=[out_shape] * 2,
+            compiler_params=LIMIT,
+            name=name,
+        )(arg, weights)
+
+    def pair_sum(keep, recv):
+        out_shape = jax.ShapeDtypeStruct(keep.shape[1:], f32)
+        return pl.pallas_call(
+            pair_sum_kernel,
+            in_specs=[VMEM] * 2,
+            out_specs=[VMEM] * 2,
+            out_shape=[out_shape] * 2,
+            compiler_params=LIMIT,
+            name="pair_sum",
+        )(keep, recv)
+
+    give_in, keep_in = project(activations, in_factor.T, True, "project_in")
+    give_in, keep_in, out_grads = lax.optimization_barrier((give_in, keep_in, out_grads))
+    recv_in = swap(give_in, 0)
+    give_out, keep_out = project(out_grads.T, out_factor.T, False, "project_out")
+    recv_out = swap(give_out, 0)
+    keep_in, give_in = pair_sum(keep_in, recv_in)
+    recv_in = swap(give_in, 1)
+    keep_out, give_out = pair_sum(keep_out, recv_out)
+    recv_out = swap(give_out, 1)
     near_sum = pl.pallas_call(
-        sum_kernel,
-        in_specs=[VMEM],
-        out_specs=VMEM,
-        out_shape=jax.ShapeDtypeStruct((len(far[0]), rank, LANES), f32),
+        near_sum_kernel,
+        in_specs=[VMEM] * 4,
+        out_specs=VMEM,
+        out_shape=jax.ShapeDtypeStruct((slices, rank, LANES), f32),
         compiler_params=LIMIT,
         name="near_sum",
-    )(near_parts.reshape(len(near[0]), len(far[0]), rank, LANES))
+    )(keep_in, recv_in, keep_out, recv_out)
     parts = lax.all_to_all(near_sum, "fsdp", 0, 0, tiled=True, axis_index_groups=far)
 
     outer = pl.pallas_call(
@@ -164,19 +207,26 @@
     )(parts)
     partials = lax.all_to_all(outer, "fsdp", 0, 0, tiled=True)
 
-    send, scores_t = pl.pallas_call(
-        functools.partial(scores_kernel, 1.0 / math.sqrt(LEN), 1.0 / math.sqrt(features)),
-        in_specs=[VMEM, VMEM],
+    phi, send = pl.pallas_call(
+        functools.partial(features_kernel, 1.0 / math.sqrt(LEN), ex_dev),
+        in_specs=[VMEM],
         out_specs=[VMEM, VMEM],
         out_shape=[
+            jax.ShapeDtypeStruct((ex_dev * feature_rows, LANES), f32),
             jax.ShapeDtypeStruct((ex_count, 2 * ex_dev, LANES), f32),
-            jax.ShapeDtypeStruct((ex_dev, tests), f32),
         ],
-        scratch_shapes=[pltpu.VMEM((ex_dev * feature_rows, LANES), f32)],
+        compiler_params=LIMIT,
+        name="features",
+    )(partials)
+    recv = lax.all_to_all(send, "ex", 0, 0, tiled=True)
+    scores_t = pl.pallas_call(
+        functools.partial(scores_kernel, 1.0 / math.sqrt(features)),
+        in_specs=[VMEM, VMEM],
+        out_specs=VMEM,
+        out_shape=jax.ShapeDtypeStruct((ex_dev, tests), f32),
         compiler_params=LIMIT,
         name="scores",
-    )(partials, test_features)
-    recv = lax.all_to_all(send, "ex", 0, 0, tiled=True)
+    )(phi, test_features)
 
     kernel = pl.pallas_call(
         functools.partial(tile_kernel, ex_dev * ex_count),

time: 95.1 us -> 90.3 us (0.950)
  blocking collectives: 86 us -> 38.1 us
  starting transfers between devices: 0 us -> 26 us
  waiting for transfers between devices: 0 us -> 16.6 us
    all_to_all x2 -> x0, blocking collectives: 41.7 us -> none  [the longest x1 21.7 us: shards(): recv = lax.all_to_all(send, 'ex', 0, 0, tiled=True)]
    ppermute x0 -> x4, starting transfers between devices: none -> 13.6 us  [swap(): return lax.ppermute(value, ('fsdp', 'ex'), pairs)]
    all_to_all x0 -> x1, starting transfers between devices: none -> 12.4 us  [shards(): recv = lax.all_to_all(send, 'ex', 0, 0, tiled=True)]
    all_to_all x0 -> x1, waiting for transfers between devices: none -> 8.88 us  [shards(): recv = lax.all_to_all(send, 'ex', 0, 0, tiled=True)]
    ppermute x0 -> x4, waiting for transfers between devices: none -> 7.73 us  [swap(): return lax.ppermute(value, ('fsdp', 'ex'), pairs)]
    all_to_all x1, blocking collectives: 23.3 us -> 17.5 us  [shards(): lax.all_to_all(near_sum, 'fsdp', 0, 0, tiled=True, axis_index_groups=far)]
    pallas_call x3 -> x7, Pallas kernels: 2.46 us -> 2.75 us  [the longest x2 1.06 us: project(): pl.pallas_call(functools.partial(project_kernel, along_rows, ex_count), i...]
  transfers between devices with their start and end apart: 0 -> 5, of which waited for: 0 -> 4; matrix products, arithmetic and copies ran while one was open for 0% -> 0% of each run, Pallas kernels for 0% -> 2%
where the time goes in v4:
time: 90.3 us; the launch traced here: 89.8 us
  blocking collectives  38.1 us (42%)
  starting transfers between devices  26 us (29%)
  waiting for transfers between devices  16.6 us (18%)
  local copies, waits for them, and re-layouts  4.47 us (5%)
  Pallas kernels  3.89 us (4%)
    all_to_all x1, blocking collectives, shards(): partials = lax.all_to_all(outer, 'fsdp', 0, 0, tiled=True)  20.6 us
    all_to_all x1, blocking collectives, shards(): lax.all_to_all(near_sum, 'fsdp', 0, 0, tiled=True, axis_index_groups=far)  17.5 us
    ppermute x4, starting transfers between devices, swap(): return lax.ppermute(value, ('fsdp', 'ex'), pairs)  13.6 us
    all_to_all x1, starting transfers between devices, shards(): recv = lax.all_to_all(send, 'ex', 0, 0, tiled=True)  12.4 us
    all_to_all x1, waiting for transfers between devices, shards(): recv = lax.all_to_all(send, 'ex', 0, 0, tiled=True)  8.88 us
    ppermute x4, waiting for transfers between devices, swap(): return lax.ppermute(value, ('fsdp', 'ex'), pairs)  7.73 us
    unnamed x10, local copies, waits for them, and re-layouts  4.47 us
  transfers between devices with their start and end apart: 5, of which 4 were waited for; matrix products, arithmetic and copies ran while one was open for 0% of the time, Pallas kernels for 2%

profile of v4, /device:TPU:1, one launch (start us, length us, event | category | flops | bytes accessed | tf_op | source)
XLA Modules:
  0.0 89.8 jit_solution(2636481008083902867)
XLA Ops:
  0.6 0.0 copy-start.1
  0.6 1.2 %copy-done.1 = bf16[4096,128]{1,0:T(8,128)(2,1)S(1)} copy-done((bf16[4096,128]{1,0:T(8,128)(2,1)S(1)}, bf16[4096,128]{1,0:T(8,128)(2,1)}, u32[]{:S(2)}) %copy-start.1) | copy-done | bytes 1048600
  1.9 0.0 copy-start.4
  1.9 0.7 copy-done.4
  2.6 0.5 project_in.1
  3.1 4.8 %collective-permute-start = (f32[2,8,64,128]{3,2,1,0:T(8,128)S(1)}, f32[2,8,64,128]{3,2,1,0:T(8,128)S(1)}, u32[]{:S(2)}, u32[]{:S(2)}) collective-permute-start(f32[2,8,64,128]{3,2,1,0:T(8,128)S(1)} %get-tuple-element.18), channel_id=1, source_target_pairs={{0,64},{16,80},{64,0},{80,16},{32,96},{48,112},{96,32},{112,48},{1... | collective-permute-start | bytes 1572872 | tf_op jit(solution)/shard_map/ppermute | solution.py:156
  7.9 0.0 copy-start
  7.9 1.8 %copy-done = bf16[4096,344]{0,1:T(8,128)(2,1)S(1)} copy-done((bf16[4096,344]{0,1:T(8,128)(2,1)S(1)}, bf16[4096,344]{0,1:T(8,128)(2,1)}, u32[]{:S(2)}) %copy-start) | copy-done | bytes 2818072
  9.7 0.0 copy-start.3
  9.7 0.7 copy-done.3
  10.4 0.6 project_out.1
  11.0 0.0 copy-start.2
  11.0 2.1 %collective-permute-start.2 = (f32[2,8,32,128]{3,2,1,0:T(8,128)S(1)}, f32[2,8,32,128]{3,2,1,0:T(8,128)S(1)}, u32[]{:S(2)}, u32[]{:S(2)}) collective-permute-start(f32[2,8,32,128]{3,2,1,0:T(8,128)S(1)} %get-tuple-element.23), channel_id=1, source_target_pairs={{0,64},{16,80},{64,0},{80,16},{32,96},{48,112},{96,32},{112,48},{1... | collective-permute-start | bytes 786440 | tf_op jit(solution)/shard_map/ppermute | solution.py:156
  13.1 1.4 %collective-permute-done.recv_ref = f32[2,8,64,128]{3,2,1,0:T(8,128)S(1)} collective-permute-done((f32[2,8,64,128]{3,2,1,0:T(8,128)S(1)}, f32[2,8,64,128]{3,2,1,0:T(8,128)S(1)}, u32[]{:S(2)}, u32[]{:S(2)}) %collective-permute-start) | collective-permute-done | bytes 524320 | tf_op jit(solution)/shard_map/ppermute | solution.py:156
  14.4 0.1 pair_sum.2
  14.5 3.5 %collective-permute-start.1 = (f32[8,64,128]{2,1,0:T(8,128)S(1)}, f32[8,64,128]{2,1,0:T(8,128)S(1)}, u32[]{:S(2)}, u32[]{:S(2)}) collective-permute-start(f32[8,64,128]{2,1,0:T(8,128)S(1)} %get-tuple-element.20), channel_id=1, source_target_pairs={{0,16},{16,0},{64,80},{80,64},{32,48},{48,32},{96,112},{112,96},{1... | collective-permute-start | bytes 786440 | tf_op jit(solution)/shard_map/ppermute | solution.py:156
  18.0 0.6 collective-permute-done.2.recv_ref
  18.6 3.2 %collective-permute-start.3 = (f32[8,32,128]{2,1,0:T(8,128)S(1)}, f32[8,32,128]{2,1,0:T(8,128)S(1)}, u32[]{:S(2)}, u32[]{:S(2)}) collective-permute-start(f32[8,32,128]{2,1,0:T(8,128)S(1)} %get-tuple-element.25), channel_id=1, source_target_pairs={{0,16},{16,0},{64,80},{80,64},{32,48},{48,32},{96,112},{112,96},{1... | collective-permute-start | bytes 393224 | tf_op jit(solution)/shard_map/ppermute | solution.py:156
  21.8 5.8 %collective-permute-done.3.recv_out_ref = f32[8,32,128]{2,1,0:T(8,128)S(1)} collective-permute-done((f32[8,32,128]{2,1,0:T(8,128)S(1)}, f32[8,32,128]{2,1,0:T(8,128)S(1)}, u32[]{:S(2)}, u32[]{:S(2)}) %collective-permute-start.3) | collective-permute-done | bytes 131104 | tf_op jit(solution)/shard_map/ppermute | solution.py:156
  27.6 0.0 collective-permute-done.1.recv_in_ref
  27.7 17.5 %all_to_all.15.parts_ref = f32[8,96,128]{2,1,0:T(8,128)S(1)} all-to-all(f32[8,96,128]{2,1,0:T(8,128)S(1)} %near_sum.1), channel_id=1, replica_groups={{0,32,128,160,256,288,384,416},{16,48,144,176,272,304,400,432},{64,96,1..., dimensions={0} | all-to-all | bytes 786432 | tf_op jit(solution)/shard_map/all_to_all | solution.py:197
  45.2 0.3 outer.1
  45.5 20.6 %all_to_all.16.parts_ref = f32[32,16,128]{2,1,0:T(8,128)S(1)} all-to-all(f32[32,16,128]{2,1,0:T(8,128)S(1)} %outer.1), channel_id=1, replica_groups=mesh['fsdp'=32,'ex'=16] {'fsdp'}, dimensions={0} | all-to-all | bytes 524288 | tf_op jit(solution)/shard_map/all_to_all | solution.py:208
  66.1 0.7 features.1
  66.8 12.4 %all-to-all-start.2 = ((f32[16,8,128]{2,1,0:T(8,128)}), f32[16,8,128]{2,1,0:T(8,128)S(1)}, u32[]{:S(2)}, u32[]{:S(2)}) async-start(f32[16,8,128]{2,1,0:T(8,128)} %get-tuple-element.26), calls=%async_computation.2 | async-start | bytes 131072 | tf_op jit(solution)/shard_map/all_to_all | solution.py:221
  79.2 0.0 copy-done.2
  79.2 0.8 scores.1
  80.0 8.9 %all-to-all-done.2.recv_ref = f32[16,8,128]{2,1,0:T(8,128)S(1)} async-done(((f32[16,8,128]{2,1,0:T(8,128)}), f32[16,8,128]{2,1,0:T(8,128)S(1)}, u32[]{:S(2)}, u32[]{:S(2)}) %all-to-all-start.2) | async-done | bytes 65568 | tf_op jit(solution)/shard_map/all_to_all | solution.py:221
  88.9 0.9 tile.1
  (2 shorter events, 0.1 us)
Async XLA Ops:
  0.6 1.2 %copy-start.1 = (bf16[4096,128]{1,0:T(8,128)(2,1)S(1)}, bf16[4096,128]{1,0:T(8,128)(2,1)}, u32[]{:S(2)}) copy-start(bf16[4096,128]{1,0:T(8,128)(2,1)} %arg_ref.1) | copy-start | bytes 3145732
  1.9 0.7 copy-start.4
  3.1 11.4 %collective-permute-start = (f32[2,8,64,128]{3,2,1,0:T(8,128)S(1)}, f32[2,8,64,128]{3,2,1,0:T(8,128)S(1)}, u32[]{:S(2)}, u32[]{:S(2)}) collective-permute-start(f32[2,8,64,128]{3,2,1,0:T(8,128)S(1)} %get-tuple-element.18), channel_id=1, source_target_pairs={{0,64},{16,80},{64,0},{80,16},{32,96},{48,112},{96,32},{112,48},{1... | collective-permute-start | bytes 1572872 | tf_op jit(solution)/shard_map/ppermute | solution.py:156
  7.9 1.8 %copy-start = (bf16[4096,344]{0,1:T(8,128)(2,1)S(1)}, bf16[4096,344]{0,1:T(8,128)(2,1)}, u32[]{:S(2)}) copy-start(bf16[4096,344]{0,1:T(8,128)(2,1)} %param.6) | copy-start | bytes 8454148
  9.7 0.7 copy-start.3
  11.0 68.2 %copy-start.2 = (f32[16,2048]{1,0:T(8,128)S(1)}, f32[16,2048]{1,0:T(8,128)}, u32[]{:S(2)}) copy-start(f32[16,2048]{1,0:T(8,128)} %test_ref.1) | copy-start | bytes 393220
  11.0 7.6 %collective-permute-start.2 = (f32[2,8,32,128]{3,2,1,0:T(8,128)S(1)}, f32[2,8,32,128]{3,2,1,0:T(8,128)S(1)}, u32[]{:S(2)}, u32[]{:S(2)}) collective-permute-start(f32[2,8,32,128]{3,2,1,0:T(8,128)S(1)} %get-tuple-element.23), channel_id=1, source_target_pairs={{0,64},{16,80},{64,0},{80,16},{32,96},{48,112},{96,32},{112,48},{1... | collective-permute-start | bytes 786440 | tf_op jit(solution)/shard_map/ppermute | solution.py:156
  14.5 13.1 %collective-permute-start.1 = (f32[8,64,128]{2,1,0:T(8,128)S(1)}, f32[8,64,128]{2,1,0:T(8,128)S(1)}, u32[]{:S(2)}, u32[]{:S(2)}) collective-permute-start(f32[8,64,128]{2,1,0:T(8,128)S(1)} %get-tuple-element.20), channel_id=1, source_target_pairs={{0,16},{16,0},{64,80},{80,64},{32,48},{48,32},{96,112},{112,96},{1... | collective-permute-start | bytes 786440 | tf_op jit(solution)/shard_map/ppermute | solution.py:156
  18.6 9.0 %collective-permute-start.3 = (f32[8,32,128]{2,1,0:T(8,128)S(1)}, f32[8,32,128]{2,1,0:T(8,128)S(1)}, u32[]{:S(2)}, u32[]{:S(2)}) collective-permute-start(f32[8,32,128]{2,1,0:T(8,128)S(1)} %get-tuple-element.25), channel_id=1, source_target_pairs={{0,16},{16,0},{64,80},{80,64},{32,48},{48,32},{96,112},{112,96},{1... | collective-permute-start | bytes 393224 | tf_op jit(solution)/shard_map/ppermute | solution.py:156
  66.8 22.1 %all-to-all-start.2 = ((f32[16,8,128]{2,1,0:T(8,128)}), f32[16,8,128]{2,1,0:T(8,128)S(1)}, u32[]{:S(2)}, u32[]{:S(2)}) async-start(f32[16,8,128]{2,1,0:T(8,128)} %get-tuple-element.26), calls=%async_computation.2 | async-start | bytes 131072 | tf_op jit(solution)/shard_map/all_to_all | solution.py:221

commit v5 on v4

--- a/solution.py
+++ b/solution.py
@@ -82,36 +82,31 @@
     out_ref[...] = jnp.broadcast_to(dense[None], out_ref.shape)
 
 
-def features_kernel(factor_scale, ex_dev, parts_ref, phi_ref, send_ref):
+def features_kernel(factor_scale, score_scale, parts_ref, test_ref, send_ref, scores_ref, phi_ref):
     sources, rows, _ = parts_ref.shape
+    ex_dev, tests = scores_ref.shape
+    weighted = []
     for x in range(ex_dev):
         phi = sum(parts_ref[f] for f in range(sources) if block_place(f) == x) * factor_scale
         phi_ref[x * rows : (x + 1) * rows, :] = phi
+        acc = jnp.zeros((tests, LANES), jnp.float32)
+        for r in range(rows):
+            acc = acc + test_ref[:, r * LANES : (r + 1) * LANES] * phi[r : r + 1, :]
+        weighted.append(acc)
     me = lax.axis_index("fsdp")
     own = phi_ref[pl.ds(me // 2, ex_dev, stride=rows), :]
     own = jnp.where(me % 2 == 0, own, pltpu.roll(own, LANES // 2, 1))
     for r in range(rows):
         send_ref[r, :ex_dev, :] = phi_ref[pl.ds(r, ex_dev, stride=rows), :]
         send_ref[r, ex_dev:, :] = own
-
-
-def scores_kernel(score_scale, phi_ref, test_ref, scores_ref):
-    ex_dev, tests = scores_ref.shape
-    rows = phi_ref.shape[0] // ex_dev
-    weighted = []
-    for x in range(ex_dev):
-        phi = phi_ref[x * rows : (x + 1) * rows, :]
-        acc = jnp.zeros((tests, LANES), jnp.float32)
-        for r in range(rows):
-            acc = acc + test_ref[:, r * LANES : (r + 1) * LANES] * phi[r : r + 1, :]
-        weighted.append(acc)
     ones = jnp.ones((8, LANES), jnp.float32)
     sums = nt_dot(ones, jnp.concatenate(weighted, axis=0), precision=HIGHEST) * score_scale
     for x in range(ex_dev):
         scores_ref[x : x + 1, :] = sums[0:1, x * tests : (x + 1) * tests]
 
 
-def tile_kernel(ex_all, recv_ref, out_ref):
+def tile_kernel(ex_all, recv_ref, scores_ref, out_ref, scores_out_ref):
+    scores_out_ref[...] = scores_ref[...]
     groups, both, _ = recv_ref.shape
     half = both // 2
     recv = recv_ref[...]
@@ -207,35 +202,28 @@
     )(parts)
     partials = lax.all_to_all(outer, "fsdp", 0, 0, tiled=True)
 
-    phi, send = pl.pallas_call(
-        functools.partial(features_kernel, 1.0 / math.sqrt(LEN), ex_dev),
-        in_specs=[VMEM],
+    scores_shape = jax.ShapeDtypeStruct((ex_dev, tests), f32)
+    send, scores = pl.pallas_call(
+        functools.partial(features_kernel, 1.0 / math.sqrt(LEN), 1.0 / math.sqrt(features)),
+        in_specs=[VMEM, VMEM],
+        out_specs=[VMEM, VMEM],
+        out_shape=[jax.ShapeDtypeStruct((ex_count, 2 * ex_dev, LANES), f32), scores_shape],
+        scratch_shapes=[pltpu.VMEM((ex_dev * feature_rows, LANES), f32)],
+        compiler_params=LIMIT,
+        name="features",
+    )(partials, test_features)
+    recv = lax.all_to_all(send, "ex", 0, 0, tiled=True)
+    kernel, scores_t = pl.pallas_call(
+        functools.partial(tile_kernel, ex_dev * ex_count),
+        in_specs=[VMEM, VMEM],
         out_specs=[VMEM, VMEM],
         out_shape=[
-            jax.ShapeDtypeStruct((ex_dev * feature_rows, LANES), f32),
-            jax.ShapeDtypeStruct((ex_count, 2 * ex_dev, LANES), f32),
+            jax.ShapeDtypeStruct((features // fsdp_count, features // ex_count), f32),
+            scores_shape,
         ],
         compiler_params=LIMIT,
-        name="features",
-    )(partials)
-    recv = lax.all_to_all(send, "ex", 0, 0, tiled=True)
-    scores_t = pl.pallas_call(
-        functools.partial(scores_kernel, 1.0 / math.sqrt(features)),
-        in_specs=[VMEM, VMEM],
-        out_specs=VMEM,
-        out_shape=jax.ShapeDtypeStruct((ex_dev, tests), f32),
-        compiler_params=LIMIT,
-        name="scores",
-    )(phi, test_features)
-
-    kernel = pl.pallas_call(
-        functools.partial(tile_kernel, ex_dev * ex_count),
-        in_specs=[VMEM],
-        out_specs=VMEM,
-        out_shape=jax.ShapeDtypeStruct((features // fsdp_count, features // ex_count), f32),
-        compiler_params=LIMIT,
         name="tile",
-    )(recv)
+    )(recv, scores)
     return (kernel, scores_t.T)
 
 

time: 90.3 us -> 89.6 us (level)
  blocking collectives: 38.1 us -> 60 us
  starting transfers between devices: 26 us -> 13.6 us
  waiting for transfers between devices: 16.6 us -> 7.73 us
  Pallas kernels: 3.89 us -> 2.61 us
    all_to_all x0 -> x1, blocking collectives: none -> 21.9 us  [shards(): recv = lax.all_to_all(send, 'ex', 0, 0, tiled=True)]
    all_to_all x1 -> x0, starting transfers between devices: 12.4 us -> none  [shards(): recv = lax.all_to_all(send, 'ex', 0, 0, tiled=True)]
    all_to_all x1 -> x0, waiting for transfers between devices: 8.88 us -> none  [shards(): recv = lax.all_to_all(send, 'ex', 0, 0, tiled=True)]
    pallas_call x2 -> x1, Pallas kernels: 1.56 us -> 0.28 us  [shards(): pl.pallas_call(functools.partial(features_kernel, 1.0 / math.sqrt(LEN), 1...]
  transfers between devices with their start and end apart: 5 -> 4, of which waited for: 4 -> 3; matrix products, arithmetic and copies ran while one was open for 0% -> 0% of each run, Pallas kernels for 2% -> 1%
where the time goes in v5:
time: 89.6 us; the launch traced here: 89.1 us
  blocking collectives  60 us (67%)
  starting transfers between devices  13.6 us (15%)
  waiting for transfers between devices  7.73 us (9%)
  local copies, waits for them, and re-layouts  4.47 us (5%)
  Pallas kernels  2.61 us (3%)
    all_to_all x1, blocking collectives, shards(): recv = lax.all_to_all(send, 'ex', 0, 0, tiled=True)  21.9 us
    all_to_all x1, blocking collectives, shards(): partials = lax.all_to_all(outer, 'fsdp', 0, 0, tiled=True)  20.6 us
    all_to_all x1, blocking collectives, shards(): lax.all_to_all(near_sum, 'fsdp', 0, 0, tiled=True, axis_index_groups=far)  17.5 us
    ppermute x4, starting transfers between devices, swap(): return lax.ppermute(value, ('fsdp', 'ex'), pairs)  13.6 us
    ppermute x4, waiting for transfers between devices, swap(): return lax.ppermute(value, ('fsdp', 'ex'), pairs)  7.73 us
    unnamed x10, local copies, waits for them, and re-layouts  4.47 us
  transfers between devices with their start and end apart: 4, of which 3 were waited for; matrix products, arithmetic and copies ran while one was open for 0% of the time, Pallas kernels for 1%

profile of v5, /device:TPU:1, one launch (start us, length us, event | category | flops | bytes accessed | tf_op | source)
XLA Modules:
  0.0 89.1 jit_solution(7272233039533891933)
XLA Ops:
  0.6 0.0 copy-start.1
  0.6 1.2 %copy-done.1 = bf16[4096,128]{1,0:T(8,128)(2,1)S(1)} copy-done((bf16[4096,128]{1,0:T(8,128)(2,1)S(1)}, bf16[4096,128]{1,0:T(8,128)(2,1)}, u32[]{:S(2)}) %copy-start.1) | copy-done | bytes 1048600
  1.9 0.0 copy-start.4
  1.9 0.7 copy-done.4
  2.6 0.5 project_in.1
  3.1 4.8 %collective-permute-start = (f32[2,8,64,128]{3,2,1,0:T(8,128)S(1)}, f32[2,8,64,128]{3,2,1,0:T(8,128)S(1)}, u32[]{:S(2)}, u32[]{:S(2)}) collective-permute-start(f32[2,8,64,128]{3,2,1,0:T(8,128)S(1)} %get-tuple-element.20), channel_id=1, source_target_pairs={{0,64},{16,80},{64,0},{80,16},{32,96},{48,112},{96,32},{112,48},{1... | collective-permute-start | bytes 1572872 | tf_op jit(solution)/shard_map/ppermute | solution.py:151
  7.9 0.0 copy-start
  7.9 1.8 %copy-done = bf16[4096,344]{0,1:T(8,128)(2,1)S(1)} copy-done((bf16[4096,344]{0,1:T(8,128)(2,1)S(1)}, bf16[4096,344]{0,1:T(8,128)(2,1)}, u32[]{:S(2)}) %copy-start) | copy-done | bytes 2818072
  9.7 0.0 copy-start.3
  9.7 0.7 copy-done.3
  10.4 0.6 project_out.1
  11.0 0.0 copy-start.2
  11.0 2.1 %collective-permute-start.2 = (f32[2,8,32,128]{3,2,1,0:T(8,128)S(1)}, f32[2,8,32,128]{3,2,1,0:T(8,128)S(1)}, u32[]{:S(2)}, u32[]{:S(2)}) collective-permute-start(f32[2,8,32,128]{3,2,1,0:T(8,128)S(1)} %get-tuple-element.25), channel_id=1, source_target_pairs={{0,64},{16,80},{64,0},{80,16},{32,96},{48,112},{96,32},{112,48},{1... | collective-permute-start | bytes 786440 | tf_op jit(solution)/shard_map/ppermute | solution.py:151
  13.1 1.4 %collective-permute-done.recv_ref = f32[2,8,64,128]{3,2,1,0:T(8,128)S(1)} collective-permute-done((f32[2,8,64,128]{3,2,1,0:T(8,128)S(1)}, f32[2,8,64,128]{3,2,1,0:T(8,128)S(1)}, u32[]{:S(2)}, u32[]{:S(2)}) %collective-permute-start) | collective-permute-done | bytes 524320 | tf_op jit(solution)/shard_map/ppermute | solution.py:151
  14.4 0.1 pair_sum.2
  14.5 3.5 %collective-permute-start.1 = (f32[8,64,128]{2,1,0:T(8,128)S(1)}, f32[8,64,128]{2,1,0:T(8,128)S(1)}, u32[]{:S(2)}, u32[]{:S(2)}) collective-permute-start(f32[8,64,128]{2,1,0:T(8,128)S(1)} %get-tuple-element.22), channel_id=1, source_target_pairs={{0,16},{16,0},{64,80},{80,64},{32,48},{48,32},{96,112},{112,96},{1... | collective-permute-start | bytes 786440 | tf_op jit(solution)/shard_map/ppermute | solution.py:151
  18.0 0.6 collective-permute-done.2.recv_ref
  18.6 3.2 %collective-permute-start.3 = (f32[8,32,128]{2,1,0:T(8,128)S(1)}, f32[8,32,128]{2,1,0:T(8,128)S(1)}, u32[]{:S(2)}, u32[]{:S(2)}) collective-permute-start(f32[8,32,128]{2,1,0:T(8,128)S(1)} %get-tuple-element.27), channel_id=1, source_target_pairs={{0,16},{16,0},{64,80},{80,64},{32,48},{48,32},{96,112},{112,96},{1... | collective-permute-start | bytes 393224 | tf_op jit(solution)/shard_map/ppermute | solution.py:151
  21.8 5.8 %collective-permute-done.3.recv_out_ref = f32[8,32,128]{2,1,0:T(8,128)S(1)} collective-permute-done((f32[8,32,128]{2,1,0:T(8,128)S(1)}, f32[8,32,128]{2,1,0:T(8,128)S(1)}, u32[]{:S(2)}, u32[]{:S(2)}) %collective-permute-start.3) | collective-permute-done | bytes 131104 | tf_op jit(solution)/shard_map/ppermute | solution.py:151
  27.6 0.0 collective-permute-done.1.recv_in_ref
  27.7 17.5 %all_to_all.15.parts_ref = f32[8,96,128]{2,1,0:T(8,128)S(1)} all-to-all(f32[8,96,128]{2,1,0:T(8,128)S(1)} %near_sum.1), channel_id=1, replica_groups={{0,32,128,160,256,288,384,416},{16,48,144,176,272,304,400,432},{64,96,1..., dimensions={0} | all-to-all | bytes 786432 | tf_op jit(solution)/shard_map/all_to_all | solution.py:192
  45.2 0.3 outer.1
  45.5 20.6 %all_to_all.16.parts_ref = f32[32,16,128]{2,1,0:T(8,128)S(1)} all-to-all(f32[32,16,128]{2,1,0:T(8,128)S(1)} %outer.1), channel_id=1, replica_groups=mesh['fsdp'=32,'ex'=16] {'fsdp'}, dimensions={0} | all-to-all | bytes 524288 | tf_op jit(solution)/shard_map/all_to_all | solution.py:203
  66.1 0.0 copy-done.2
  66.1 0.3 features.1
  66.4 21.9 %all_to_all.17.recv_ref = f32[16,8,128]{2,1,0:T(8,128)S(1)} all-to-all(f32[16,8,128]{2,1,0:T(8,128)S(1)} %get-tuple-element.28), channel_id=1, replica_groups=mesh['fsdp'=32,'ex'=16] {'ex'}, dimensions={0} | all-to-all | bytes 131072 | tf_op jit(solution)/shard_map/all_to_all | solution.py:215
  88.3 0.9 tile.1
  (2 shorter events, 0.1 us)
Async XLA Ops:
  0.6 1.2 %copy-start.1 = (bf16[4096,128]{1,0:T(8,128)(2,1)S(1)}, bf16[4096,128]{1,0:T(8,128)(2,1)}, u32[]{:S(2)}) copy-start(bf16[4096,128]{1,0:T(8,128)(2,1)} %arg_ref.1) | copy-start | bytes 3145732
  1.9 0.7 copy-start.4
  3.1 11.4 %collective-permute-start = (f32[2,8,64,128]{3,2,1,0:T(8,128)S(1)}, f32[2,8,64,128]{3,2,1,0:T(8,128)S(1)}, u32[]{:S(2)}, u32[]{:S(2)}) collective-permute-start(f32[2,8,64,128]{3,2,1,0:T(8,128)S(1)} %get-tuple-element.20), channel_id=1, source_target_pairs={{0,64},{16,80},{64,0},{80,16},{32,96},{48,112},{96,32},{112,48},{1... | collective-permute-start | bytes 1572872 | tf_op jit(solution)/shard_map/ppermute | solution.py:151
  7.9 1.8 %copy-start = (bf16[4096,344]{0,1:T(8,128)(2,1)S(1)}, bf16[4096,344]{0,1:T(8,128)(2,1)}, u32[]{:S(2)}) copy-start(bf16[4096,344]{0,1:T(8,128)(2,1)} %param.6) | copy-start | bytes 8454148
  9.7 0.7 copy-start.3
  11.0 55.1 %copy-start.2 = (f32[16,2048]{1,0:T(8,128)S(1)}, f32[16,2048]{1,0:T(8,128)}, u32[]{:S(2)}) copy-start(f32[16,2048]{1,0:T(8,128)} %test_ref.1) | copy-start | bytes 393220
  11.0 7.6 %collective-permute-start.2 = (f32[2,8,32,128]{3,2,1,0:T(8,128)S(1)}, f32[2,8,32,128]{3,2,1,0:T(8,128)S(1)}, u32[]{:S(2)}, u32[]{:S(2)}) collective-permute-start(f32[2,8,32,128]{3,2,1,0:T(8,128)S(1)} %get-tuple-element.25), channel_id=1, source_target_pairs={{0,64},{16,80},{64,0},{80,16},{32,96},{48,112},{96,32},{112,48},{1... | collective-permute-start | bytes 786440 | tf_op jit(solution)/shard_map/ppermute | solution.py:151
  14.5 13.1 %collective-permute-start.1 = (f32[8,64,128]{2,1,0:T(8,128)S(1)}, f32[8,64,128]{2,1,0:T(8,128)S(1)}, u32[]{:S(2)}, u32[]{:S(2)}) collective-permute-start(f32[8,64,128]{2,1,0:T(8,128)S(1)} %get-tuple-element.22), channel_id=1, source_target_pairs={{0,16},{16,0},{64,80},{80,64},{32,48},{48,32},{96,112},{112,96},{1... | collective-permute-start | bytes 786440 | tf_op jit(solution)/shard_map/ppermute | solution.py:151
  18.6 9.0 %collective-permute-start.3 = (f32[8,32,128]{2,1,0:T(8,128)S(1)}, f32[8,32,128]{2,1,0:T(8,128)S(1)}, u32[]{:S(2)}, u32[]{:S(2)}) collective-permute-start(f32[8,32,128]{2,1,0:T(8,128)S(1)} %get-tuple-element.27), channel_id=1, source_target_pairs={{0,16},{16,0},{64,80},{80,64},{32,48},{48,32},{96,112},{112,96},{1... | collective-permute-start | bytes 393224 | tf_op jit(solution)/shard_map/ppermute | solution.py:151

commit v6 on v5

--- a/solution.py
+++ b/solution.py
@@ -10,6 +10,8 @@
 
 LEN = 1024
 LANES = 128
+EX_ORDER = [10, 5, 12, 9, 14, 3, 0, 8, 13, 2, 15, 6, 11, 1, 4, 7]
+GATHER_ORDER = [9, 24, 14, 10, 28, 1, 5, 3, 22, 21, 13, 12, 23, 16, 27, 6, 7, 29, 8, 25, 0, 26, 2, 30, 20, 31, 19, 11, 4, 17, 18, 15]
 Z = 4
 LIMIT = pltpu.CompilerParams(vmem_limit_bytes=16 * 2**20)
 HIGHEST = lax.Precision.HIGHEST
@@ -87,7 +89,7 @@
     ex_dev, tests = scores_ref.shape
     weighted = []
     for x in range(ex_dev):
-        phi = sum(parts_ref[f] for f in range(sources) if block_place(f) == x) * factor_scale
+        phi = sum(parts_ref[f] for f in range(sources) if block_place(GATHER_ORDER[f]) == x) * factor_scale
         phi_ref[x * rows : (x + 1) * rows, :] = phi
         acc = jnp.zeros((tests, LANES), jnp.float32)
         for r in range(rows):
@@ -96,9 +98,9 @@
     me = lax.axis_index("fsdp")
     own = phi_ref[pl.ds(me // 2, ex_dev, stride=rows), :]
     own = jnp.where(me % 2 == 0, own, pltpu.roll(own, LANES // 2, 1))
-    for r in range(rows):
-        send_ref[r, :ex_dev, :] = phi_ref[pl.ds(r, ex_dev, stride=rows), :]
-        send_ref[r, ex_dev:, :] = own
+    for k, r in enumerate(EX_ORDER):
+        send_ref[k, :ex_dev, :] = phi_ref[pl.ds(r, ex_dev, stride=rows), :]
+        send_ref[k, ex_dev:, :] = own
     ones = jnp.ones((8, LANES), jnp.float32)
     sums = nt_dot(ones, jnp.concatenate(weighted, axis=0), precision=HIGHEST) * score_scale
     for x in range(ex_dev):
@@ -200,7 +202,7 @@
         compiler_params=LIMIT,
         name="outer",
     )(parts)
-    partials = lax.all_to_all(outer, "fsdp", 0, 0, tiled=True)
+    partials = lax.all_to_all(outer, "fsdp", 0, 0, tiled=True, axis_index_groups=[GATHER_ORDER])
 
     scores_shape = jax.ShapeDtypeStruct((ex_dev, tests), f32)
     send, scores = pl.pallas_call(
@@ -212,7 +214,7 @@
         compiler_params=LIMIT,
         name="features",
     )(partials, test_features)
-    recv = lax.all_to_all(send, "ex", 0, 0, tiled=True)
+    recv = lax.all_to_all(send, "ex", 0, 0, tiled=True, axis_index_groups=[EX_ORDER])
     kernel, scores_t = pl.pallas_call(
         functools.partial(tile_kernel, ex_dev * ex_count),
         in_specs=[VMEM, VMEM],

time: 89.6 us -> 81.7 us (0.912)
  blocking collectives: 60 us -> 52 us
    all_to_all x2, blocking collectives: 42.5 us -> 34.5 us  [the longest x1 17.7 us: shards(): lax.all_to_all(outer, 'fsdp', 0, 0, tiled=True, axis_index_groups=[GATHER...]
where the time goes in v6:
time: 81.7 us; the launch traced here: 81.2 us
  blocking collectives  52 us (64%)
  starting transfers between devices  13.6 us (17%)
  waiting for transfers between devices  7.73 us (9%)
  local copies, waits for them, and re-layouts  4.47 us (5%)
  Pallas kernels  2.61 us (3%)
    all_to_all x1, blocking collectives, shards(): lax.all_to_all(outer, 'fsdp', 0, 0, tiled=True, axis_index_groups=[GATHER...  17.7 us
    all_to_all x1, blocking collectives, shards(): lax.all_to_all(near_sum, 'fsdp', 0, 0, tiled=True, axis_index_groups=far)  17.5 us
    all_to_all x1, blocking collectives, shards(): lax.all_to_all(send, 'ex', 0, 0, tiled=True, axis_index_groups=[EX_ORDER])  16.8 us
    ppermute x4, starting transfers between devices, swap(): return lax.ppermute(value, ('fsdp', 'ex'), pairs)  13.6 us
    ppermute x4, waiting for transfers between devices, swap(): return lax.ppermute(value, ('fsdp', 'ex'), pairs)  7.73 us
    unnamed x10, local copies, waits for them, and re-layouts  4.47 us
  transfers between devices with their start and end apart: 4, of which 3 were waited for; matrix products, arithmetic and copies ran while one was open for 0% of the time, Pallas kernels for 1%

profile of v6, /device:TPU:1, one launch (start us, length us, event | category | flops | bytes accessed | tf_op | source)
XLA Modules:
  0.0 81.2 jit_solution(1433625549906790897)
XLA Ops:
  0.6 0.0 copy-start.1
  0.6 1.2 %copy-done.1 = bf16[4096,128]{1,0:T(8,128)(2,1)S(1)} copy-done((bf16[4096,128]{1,0:T(8,128)(2,1)S(1)}, bf16[4096,128]{1,0:T(8,128)(2,1)}, u32[]{:S(2)}) %copy-start.1) | copy-done | bytes 1048600
  1.9 0.0 copy-start.4
  1.9 0.7 copy-done.4
  2.6 0.5 project_in.1
  3.1 4.8 %collective-permute-start = (f32[2,8,64,128]{3,2,1,0:T(8,128)S(1)}, f32[2,8,64,128]{3,2,1,0:T(8,128)S(1)}, u32[]{:S(2)}, u32[]{:S(2)}) collective-permute-start(f32[2,8,64,128]{3,2,1,0:T(8,128)S(1)} %get-tuple-element.20), channel_id=1, source_target_pairs={{0,64},{16,80},{64,0},{80,16},{32,96},{48,112},{96,32},{112,48},{1... | collective-permute-start | bytes 1572872 | tf_op jit(solution)/shard_map/ppermute | solution.py:153
  7.9 0.0 copy-start
  7.9 1.8 %copy-done = bf16[4096,344]{0,1:T(8,128)(2,1)S(1)} copy-done((bf16[4096,344]{0,1:T(8,128)(2,1)S(1)}, bf16[4096,344]{0,1:T(8,128)(2,1)}, u32[]{:S(2)}) %copy-start) | copy-done | bytes 2818072
  9.7 0.0 copy-start.3
  9.7 0.7 copy-done.3
  10.4 0.6 project_out.1
  11.0 0.0 copy-start.2
  11.0 2.1 %collective-permute-start.2 = (f32[2,8,32,128]{3,2,1,0:T(8,128)S(1)}, f32[2,8,32,128]{3,2,1,0:T(8,128)S(1)}, u32[]{:S(2)}, u32[]{:S(2)}) collective-permute-start(f32[2,8,32,128]{3,2,1,0:T(8,128)S(1)} %get-tuple-element.25), channel_id=1, source_target_pairs={{0,64},{16,80},{64,0},{80,16},{32,96},{48,112},{96,32},{112,48},{1... | collective-permute-start | bytes 786440 | tf_op jit(solution)/shard_map/ppermute | solution.py:153
  13.1 1.4 %collective-permute-done.recv_ref = f32[2,8,64,128]{3,2,1,0:T(8,128)S(1)} collective-permute-done((f32[2,8,64,128]{3,2,1,0:T(8,128)S(1)}, f32[2,8,64,128]{3,2,1,0:T(8,128)S(1)}, u32[]{:S(2)}, u32[]{:S(2)}) %collective-permute-start) | collective-permute-done | bytes 524320 | tf_op jit(solution)/shard_map/ppermute | solution.py:153
  14.4 0.1 pair_sum.2
  14.5 3.5 %collective-permute-start.1 = (f32[8,64,128]{2,1,0:T(8,128)S(1)}, f32[8,64,128]{2,1,0:T(8,128)S(1)}, u32[]{:S(2)}, u32[]{:S(2)}) collective-permute-start(f32[8,64,128]{2,1,0:T(8,128)S(1)} %get-tuple-element.22), channel_id=1, source_target_pairs={{0,16},{16,0},{64,80},{80,64},{32,48},{48,32},{96,112},{112,96},{1... | collective-permute-start | bytes 786440 | tf_op jit(solution)/shard_map/ppermute | solution.py:153
  18.0 0.6 collective-permute-done.2.recv_ref
  18.6 3.2 %collective-permute-start.3 = (f32[8,32,128]{2,1,0:T(8,128)S(1)}, f32[8,32,128]{2,1,0:T(8,128)S(1)}, u32[]{:S(2)}, u32[]{:S(2)}) collective-permute-start(f32[8,32,128]{2,1,0:T(8,128)S(1)} %get-tuple-element.27), channel_id=1, source_target_pairs={{0,16},{16,0},{64,80},{80,64},{32,48},{48,32},{96,112},{112,96},{1... | collective-permute-start | bytes 393224 | tf_op jit(solution)/shard_map/ppermute | solution.py:153
  21.8 5.8 %collective-permute-done.3.recv_out_ref = f32[8,32,128]{2,1,0:T(8,128)S(1)} collective-permute-done((f32[8,32,128]{2,1,0:T(8,128)S(1)}, f32[8,32,128]{2,1,0:T(8,128)S(1)}, u32[]{:S(2)}, u32[]{:S(2)}) %collective-permute-start.3) | collective-permute-done | bytes 131104 | tf_op jit(solution)/shard_map/ppermute | solution.py:153
  27.6 0.0 collective-permute-done.1.recv_in_ref
  27.7 17.5 %all_to_all.15.parts_ref = f32[8,96,128]{2,1,0:T(8,128)S(1)} all-to-all(f32[8,96,128]{2,1,0:T(8,128)S(1)} %near_sum.1), channel_id=1, replica_groups={{0,32,128,160,256,288,384,416},{16,48,144,176,272,304,400,432},{64,96,1..., dimensions={0} | all-to-all | bytes 786432 | tf_op jit(solution)/shard_map/all_to_all | solution.py:194
  45.2 0.3 outer.1
  45.5 17.7 %all_to_all.16.parts_ref = f32[32,16,128]{2,1,0:T(8,128)S(1)} all-to-all(f32[32,16,128]{2,1,0:T(8,128)S(1)} %outer.1), channel_id=1, replica_groups={{144,384,224,160,448,16,80,48,352,336,208,192,368,256,432,96,112,464,12..., dimensions={0} | all-to-all | bytes 524288 | tf_op jit(solution)/shard_map/all_to_all | solution.py:205
  63.2 0.0 copy-done.2
  63.2 0.3 features.1
  63.4 16.8 %all_to_all.17.recv_ref = f32[16,8,128]{2,1,0:T(8,128)S(1)} all-to-all(f32[16,8,128]{2,1,0:T(8,128)S(1)} %get-tuple-element.28), channel_id=1, replica_groups={{10,5,12,9,14,3,0,8,13,2,15,6,11,1,4,7},{26,21,28,25,30,19,16,24,29,18,..., dimensions={0} | all-to-all | bytes 131072 | tf_op jit(solution)/shard_map/all_to_all | solution.py:217
  80.3 0.9 %tile.1 = (f32[64,128]{1,0:T(8,128)}, f32[4,16]{1,0:T(4,128)}) custom-call(f32[16,8,128]{2,1,0:T(8,128)S(1)} %all_to_all.17.recv_ref, f32[4,16]{1,0:T(4,128)S(1)} %get-tuple-element.29.scores_ref), custom_call_target="tpu_custom_call" | custom-call | tf_op jit(solution)/shard_map/tile/pallas_call | solution.py:218
  (2 shorter events, 0.1 us)
Async XLA Ops:
  0.6 1.2 %copy-start.1 = (bf16[4096,128]{1,0:T(8,128)(2,1)S(1)}, bf16[4096,128]{1,0:T(8,128)(2,1)}, u32[]{:S(2)}) copy-start(bf16[4096,128]{1,0:T(8,128)(2,1)} %arg_ref.1) | copy-start | bytes 3145732
  1.9 0.7 copy-start.4
  3.1 11.4 %collective-permute-start = (f32[2,8,64,128]{3,2,1,0:T(8,128)S(1)}, f32[2,8,64,128]{3,2,1,0:T(8,128)S(1)}, u32[]{:S(2)}, u32[]{:S(2)}) collective-permute-start(f32[2,8,64,128]{3,2,1,0:T(8,128)S(1)} %get-tuple-element.20), channel_id=1, source_target_pairs={{0,64},{16,80},{64,0},{80,16},{32,96},{48,112},{96,32},{112,48},{1... | collective-permute-start | bytes 1572872 | tf_op jit(solution)/shard_map/ppermute | solution.py:153
  7.9 1.8 %copy-start = (bf16[4096,344]{0,1:T(8,128)(2,1)S(1)}, bf16[4096,344]{0,1:T(8,128)(2,1)}, u32[]{:S(2)}) copy-start(bf16[4096,344]{0,1:T(8,128)(2,1)} %param.6) | copy-start | bytes 8454148
  9.7 0.7 copy-start.3
  11.0 52.1 %copy-start.2 = (f32[16,2048]{1,0:T(8,128)S(1)}, f32[16,2048]{1,0:T(8,128)}, u32[]{:S(2)}) copy-start(f32[16,2048]{1,0:T(8,128)} %test_ref.1) | copy-start | bytes 393220
  11.0 7.6 %collective-permute-start.2 = (f32[2,8,32,128]{3,2,1,0:T(8,128)S(1)}, f32[2,8,32,128]{3,2,1,0:T(8,128)S(1)}, u32[]{:S(2)}, u32[]{:S(2)}) collective-permute-start(f32[2,8,32,128]{3,2,1,0:T(8,128)S(1)} %get-tuple-element.25), channel_id=1, source_target_pairs={{0,64},{16,80},{64,0},{80,16},{32,96},{48,112},{96,32},{112,48},{1... | collective-permute-start | bytes 786440 | tf_op jit(solution)/shard_map/ppermute | solution.py:153
  14.5 13.1 %collective-permute-start.1 = (f32[8,64,128]{2,1,0:T(8,128)S(1)}, f32[8,64,128]{2,1,0:T(8,128)S(1)}, u32[]{:S(2)}, u32[]{:S(2)}) collective-permute-start(f32[8,64,128]{2,1,0:T(8,128)S(1)} %get-tuple-element.22), channel_id=1, source_target_pairs={{0,16},{16,0},{64,80},{80,64},{32,48},{48,32},{96,112},{112,96},{1... | collective-permute-start | bytes 786440 | tf_op jit(solution)/shard_map/ppermute | solution.py:153
  18.6 9.0 %collective-permute-start.3 = (f32[8,32,128]{2,1,0:T(8,128)S(1)}, f32[8,32,128]{2,1,0:T(8,128)S(1)}, u32[]{:S(2)}, u32[]{:S(2)}) collective-permute-start(f32[8,32,128]{2,1,0:T(8,128)S(1)} %get-tuple-element.27), channel_id=1, source_target_pairs={{0,16},{16,0},{64,80},{80,64},{32,48},{48,32},{96,112},{112,96},{1... | collective-permute-start | bytes 393224 | tf_op jit(solution)/shard_map/ppermute | solution.py:153

commit v7 on v6

--- a/solution.py
+++ b/solution.py
@@ -12,10 +12,12 @@
 LANES = 128
 EX_ORDER = [10, 5, 12, 9, 14, 3, 0, 8, 13, 2, 15, 6, 11, 1, 4, 7]
 GATHER_ORDER = [9, 24, 14, 10, 28, 1, 5, 3, 22, 21, 13, 12, 23, 16, 27, 6, 7, 29, 8, 25, 0, 26, 2, 30, 20, 31, 19, 11, 4, 17, 18, 15]
+FAR_ORDER = [1, 6, 5, 4, 7, 0, 2, 3]
 Z = 4
 LIMIT = pltpu.CompilerParams(vmem_limit_bytes=16 * 2**20)
 HIGHEST = lax.Precision.HIGHEST
 VMEM = pl.BlockSpec(memory_space=pltpu.VMEM)
+HBM = pl.BlockSpec(memory_space=pltpu.HBM)
 
 
 def nt_dot(a, b, **kw):
@@ -42,6 +44,21 @@
         out_ref = keep_ref if k >= 2 else give_ref
         for s in range(LEN // LANES):
             out_ref[k % 2, s] = proj[:, s * LANES : (s + 1) * LANES]
+
+
+def project_rows_kernel(kept, ex_count, arg_hbm, weights_hbm, out_ref, arg, weights, sems):
+    copies = [pltpu.make_async_copy(weights_hbm, weights, sems.at[2])]
+    for k, place in enumerate(place_order(ex_count)[2 * kept : 2 * kept + 2]):
+        own = pl.ds(pl.multiple_of(place * LEN, LEN), LEN)
+        copies.append(pltpu.make_async_copy(arg_hbm.at[own, :], arg.at[k], sems.at[k]))
+    for copy in copies:
+        copy.start()
+    copies[0].wait()
+    for k in range(2):
+        copies[1 + k].wait()
+        proj = nt_dot(weights[...], arg[k])
+        for s in range(LEN // LANES):
+            out_ref[k, s] = proj[:, s * LANES : (s + 1) * LANES]
 
 
 def block_groups(fsdp_count):
@@ -163,6 +180,21 @@
             name=name,
         )(arg, weights)
 
+    def project_rows(arg, weights, kept, name):
+        return pl.pallas_call(
+            functools.partial(project_rows_kernel, kept, ex_count),
+            in_specs=[HBM] * 2,
+            out_specs=VMEM,
+            out_shape=jax.ShapeDtypeStruct((2, slices, weights.shape[0], LANES), f32),
+            scratch_shapes=[
+                pltpu.VMEM((2, LEN, arg.shape[1]), arg.dtype),
+                pltpu.VMEM(weights.shape, weights.dtype),
+                pltpu.SemaphoreType.DMA((3,)),
+            ],
+            compiler_params=pltpu.CompilerParams(vmem_limit_bytes=53 * 2**20 if not kept else 58 * 2**20),
+            name=name,
+        )(arg, weights)
+
     def pair_sum(keep, recv):
         out_shape = jax.ShapeDtypeStruct(keep.shape[1:], f32)
         return pl.pallas_call(
@@ -174,9 +206,11 @@
             name="pair_sum",
         )(keep, recv)
 
-    give_in, keep_in = project(activations, in_factor.T, True, "project_in")
-    give_in, keep_in, out_grads = lax.optimization_barrier((give_in, keep_in, out_grads))
+    give_in = project_rows(activations, in_factor.T, 0, "project_in_give")
+    give_in, out_grads, activations = lax.optimization_barrier((give_in, out_grads, activations))
     recv_in = swap(give_in, 0)
+    keep_in = project_rows(activations, in_factor.T, 1, "project_in_keep")
+    keep_in, out_grads = lax.optimization_barrier((keep_in, out_grads))
     give_out, keep_out = project(out_grads.T, out_factor.T, False, "project_out")
     recv_out = swap(give_out, 0)
     keep_in, give_in = pair_sum(keep_in, recv_in)
@@ -191,7 +225,9 @@
         compiler_params=LIMIT,
         name="near_sum",
     )(keep_in, recv_in, keep_out, recv_out)
-    parts = lax.all_to_all(near_sum, "fsdp", 0, 0, tiled=True, axis_index_groups=far)
+    parts = lax.all_to_all(
+        near_sum, "fsdp", 0, 0, tiled=True, axis_index_groups=[[group[k] for k in FAR_ORDER] for group in far]
+    )
 
     outer = pl.pallas_call(
         functools.partial(outer_kernel, in_rank),

time: 81.7 us -> 81.1 us (level)
  local copies, waits for them, and re-layouts: 4.47 us -> 0.88 us
  Pallas kernels: 2.61 us -> 5.77 us
    pallas_call x0 -> x2, Pallas kernels: none -> 3.62 us  [project_rows(): pl.pallas_call(functools.partial(project_rows_kernel, kept, ex_count), in...]
    unnamed x10, local copies, waits for them, and re-layouts: 4.47 us -> 0.88 us
    all_to_all x1, blocking collectives: 17.5 us -> 15.9 us  [shards(): lax.all_to_all(near_sum, 'fsdp', 0, 0, tiled=True, axis_index_groups=[[gr...]
    all_to_all x1, blocking collectives: 16.8 us -> 17.8 us  [shards(): lax.all_to_all(send, 'ex', 0, 0, tiled=True, axis_index_groups=[EX_ORDER])]
  transfers between devices with their start and end apart: 4 -> 4, of which waited for: 3 -> 3; matrix products, arithmetic and copies ran while one was open for 0% -> 0% of each run, Pallas kernels for 1% -> 4%
where the time goes in v7:
time: 81.1 us; the launch traced here: 80.6 us
  blocking collectives  51.6 us (64%)
  starting transfers between devices  13.6 us (17%)
  waiting for transfers between devices  8 us (10%)
  Pallas kernels  5.77 us (7%)
  local copies, waits for them, and re-layouts  0.88 us (1%)
    all_to_all x1, blocking collectives, shards(): lax.all_to_all(outer, 'fsdp', 0, 0, tiled=True, axis_index_groups=[GATHER...  17.9 us
    all_to_all x1, blocking collectives, shards(): lax.all_to_all(send, 'ex', 0, 0, tiled=True, axis_index_groups=[EX_ORDER])  17.8 us
    all_to_all x1, blocking collectives, shards(): lax.all_to_all(near_sum, 'fsdp', 0, 0, tiled=True, axis_index_groups=[[gr...  15.9 us
    ppermute x4, starting transfers between devices, swap(): return lax.ppermute(value, ('fsdp', 'ex'), pairs)  13.6 us
    ppermute x4, waiting for transfers between devices, swap(): return lax.ppermute(value, ('fsdp', 'ex'), pairs)  8 us
    pallas_call x2, Pallas kernels, project_rows(): pl.pallas_call(functools.partial(project_rows_kernel, kept, ex_count), in...  3.62 us
  transfers between devices with their start and end apart: 4, of which 3 were waited for; matrix products, arithmetic and copies ran while one was open for 0% of the time, Pallas kernels for 4%

profile of v7, /device:TPU:1, one launch (start us, length us, event | category | flops | bytes accessed | tf_op | source)
XLA Modules:
  0.0 80.6 jit_solution(17084990210051282063)
XLA Ops:
  0.6 0.0 copy-start
  0.6 0.0 copy-start.3
  0.7 0.9 %copy-done.3 = bf16[128,64]{0,1:T(8,128)(2,1)S(1)} copy-done((bf16[128,64]{0,1:T(8,128)(2,1)S(1)}, bf16[128,64]{0,1:T(8,128)(2,1)}, u32[]{:S(2)}) %copy-start.3) | copy-done | bytes 16408
  1.5 0.0 copy-start.4
  1.5 1.4 %project_in_give.1 = f32[2,8,64,128]{3,2,1,0:T(8,128)S(1)} custom-call(bf16[4096,128]{1,0:T(8,128)(2,1)} %arg_hbm.2, bf16[64,128]{1,0:T(8,128)(2,1)S(1)} %bitcast.6), custom_call_target="tpu_custom_call" | custom-call | tf_op jit(solution)/shard_map/project_in_give/pallas_call | solution.py:184
  2.9 4.8 %collective-permute-start = (f32[2,8,64,128]{3,2,1,0:T(8,128)S(1)}, f32[2,8,64,128]{3,2,1,0:T(8,128)S(1)}, u32[]{:S(2)}, u32[]{:S(2)}) collective-permute-start(f32[2,8,64,128]{3,2,1,0:T(8,128)S(1)} %project_in_give.1), channel_id=1, source_target_pairs={{0,64},{16,80},{64,0},{80,16},{32,96},{48,112},{96,32},{112,48},{1... | collective-permute-start | bytes 1572872 | tf_op jit(solution)/shard_map/ppermute | solution.py:170
  7.8 2.2 %project_in_keep.1.keep_ref = f32[2,8,64,128]{3,2,1,0:T(8,128)} custom-call(bf16[4096,128]{1,0:T(8,128)(2,1)} %arg_hbm.2, bf16[64,128]{1,0:T(8,128)(2,1)} %bitcast.5), custom_call_target="tpu_custom_call" | custom-call | tf_op jit(solution)/shard_map/project_in_keep/pallas_call | solution.py:184
  10.0 0.0 copy-start.1
  10.0 0.0 copy-done
  10.0 0.0 copy-done.4
  10.0 0.6 project_out.1
  10.6 0.0 copy-start.2
  10.6 2.1 %collective-permute-start.2 = (f32[2,8,32,128]{3,2,1,0:T(8,128)S(1)}, f32[2,8,32,128]{3,2,1,0:T(8,128)S(1)}, u32[]{:S(2)}, u32[]{:S(2)}) collective-permute-start(f32[2,8,32,128]{3,2,1,0:T(8,128)S(1)} %get-tuple-element.25), channel_id=1, source_target_pairs={{0,64},{16,80},{64,0},{80,16},{32,96},{48,112},{96,32},{112,48},{1... | collective-permute-start | bytes 786440 | tf_op jit(solution)/shard_map/ppermute | solution.py:170
  12.7 1.6 %collective-permute-done.recv_ref = f32[2,8,64,128]{3,2,1,0:T(8,128)S(1)} collective-permute-done((f32[2,8,64,128]{3,2,1,0:T(8,128)S(1)}, f32[2,8,64,128]{3,2,1,0:T(8,128)S(1)}, u32[]{:S(2)}, u32[]{:S(2)}) %collective-permute-start) | collective-permute-done | bytes 524320 | tf_op jit(solution)/shard_map/ppermute | solution.py:170
  14.3 0.0 copy-done.1
  14.3 0.1 pair_sum.2
  14.4 3.5 %collective-permute-start.1 = (f32[8,64,128]{2,1,0:T(8,128)S(1)}, f32[8,64,128]{2,1,0:T(8,128)S(1)}, u32[]{:S(2)}, u32[]{:S(2)}) collective-permute-start(f32[8,64,128]{2,1,0:T(8,128)S(1)} %get-tuple-element.22), channel_id=1, source_target_pairs={{0,16},{16,0},{64,80},{80,64},{32,48},{48,32},{96,112},{112,96},{1... | collective-permute-start | bytes 786440 | tf_op jit(solution)/shard_map/ppermute | solution.py:170
  17.9 0.3 collective-permute-done.2.recv_ref
  18.2 3.2 %collective-permute-start.3 = (f32[8,32,128]{2,1,0:T(8,128)S(1)}, f32[8,32,128]{2,1,0:T(8,128)S(1)}, u32[]{:S(2)}, u32[]{:S(2)}) collective-permute-start(f32[8,32,128]{2,1,0:T(8,128)S(1)} %get-tuple-element.27), channel_id=1, source_target_pairs={{0,16},{16,0},{64,80},{80,64},{32,48},{48,32},{96,112},{112,96},{1... | collective-permute-start | bytes 393224 | tf_op jit(solution)/shard_map/ppermute | solution.py:170
  21.4 6.1 %collective-permute-done.3.recv_out_ref = f32[8,32,128]{2,1,0:T(8,128)S(1)} collective-permute-done((f32[8,32,128]{2,1,0:T(8,128)S(1)}, f32[8,32,128]{2,1,0:T(8,128)S(1)}, u32[]{:S(2)}, u32[]{:S(2)}) %collective-permute-start.3) | collective-permute-done | bytes 131104 | tf_op jit(solution)/shard_map/ppermute | solution.py:170
  27.5 0.0 collective-permute-done.1.recv_in_ref
  27.6 15.9 %all_to_all.15.parts_ref = f32[8,96,128]{2,1,0:T(8,128)S(1)} all-to-all(f32[8,96,128]{2,1,0:T(8,128)S(1)} %near_sum.1), channel_id=1, replica_groups={{32,384,288,256,416,0,128,160},{48,400,304,272,432,16,144,176},{96,448,..., dimensions={0} | all-to-all | bytes 786432 | tf_op jit(solution)/shard_map/all_to_all | solution.py:228
  43.5 0.3 outer.1
  43.8 17.9 %all_to_all.16.parts_ref = f32[32,16,128]{2,1,0:T(8,128)S(1)} all-to-all(f32[32,16,128]{2,1,0:T(8,128)S(1)} %outer.1), channel_id=1, replica_groups={{144,384,224,160,448,16,80,48,352,336,208,192,368,256,432,96,112,464,12..., dimensions={0} | all-to-all | bytes 524288 | tf_op jit(solution)/shard_map/all_to_all | solution.py:241
  61.7 0.0 copy-done.2
  61.7 0.3 features.1
  61.9 17.8 %all_to_all.17.recv_ref = f32[16,8,128]{2,1,0:T(8,128)S(1)} all-to-all(f32[16,8,128]{2,1,0:T(8,128)S(1)} %get-tuple-element.28), channel_id=1, replica_groups={{10,5,12,9,14,3,0,8,13,2,15,6,11,1,4,7},{26,21,28,25,30,19,16,24,29,18,..., dimensions={0} | all-to-all | bytes 131072 | tf_op jit(solution)/shard_map/all_to_all | solution.py:253
  79.7 0.9 %tile.1 = (f32[64,128]{1,0:T(8,128)}, f32[4,16]{1,0:T(4,128)}) custom-call(f32[16,8,128]{2,1,0:T(8,128)S(1)} %all_to_all.17.recv_ref, f32[4,16]{1,0:T(4,128)S(1)} %get-tuple-element.29.scores_ref), custom_call_target="tpu_custom_call" | custom-call | tf_op jit(solution)/shard_map/tile/pallas_call | solution.py:254
  (2 shorter events, 0.1 us)
Async XLA Ops:
  0.6 9.4 %copy-start = (bf16[4096,344]{0,1:T(8,128)(2,1)S(1)}, bf16[4096,344]{0,1:T(8,128)(2,1)}, u32[]{:S(2)}) copy-start(bf16[4096,344]{0,1:T(8,128)(2,1)} %param.6) | copy-start | bytes 8454148
  0.6 0.9 %copy-start.3 = (bf16[128,64]{0,1:T(8,128)(2,1)S(1)}, bf16[128,64]{0,1:T(8,128)(2,1)}, u32[]{:S(2)}) copy-start(bf16[128,64]{0,1:T(8,128)(2,1)} %param.7) | copy-start | bytes 49156
  1.5 8.5 %copy-start.4 = (bf16[344,32]{0,1:T(8,128)(2,1)S(1)}, bf16[344,32]{0,1:T(8,128)(2,1)}, u32[]{:S(2)}) copy-start(bf16[344,32]{0,1:T(8,128)(2,1)} %param.8) | copy-start | bytes 66052
  2.9 11.4 %collective-permute-start = (f32[2,8,64,128]{3,2,1,0:T(8,128)S(1)}, f32[2,8,64,128]{3,2,1,0:T(8,128)S(1)}, u32[]{:S(2)}, u32[]{:S(2)}) collective-permute-start(f32[2,8,64,128]{3,2,1,0:T(8,128)S(1)} %project_in_give.1), channel_id=1, source_target_pairs={{0,64},{16,80},{64,0},{80,16},{32,96},{48,112},{96,32},{112,48},{1... | collective-permute-start | bytes 1572872 | tf_op jit(solution)/shard_map/ppermute | solution.py:170
  10.0 4.3 %copy-start.1 = (f32[2,8,64,128]{3,2,1,0:T(8,128)S(1)}, f32[2,8,64,128]{3,2,1,0:T(8,128)}, u32[]{:S(2)}) copy-start(f32[2,8,64,128]{3,2,1,0:T(8,128)} %project_in_keep.1.keep_ref) | copy-start | bytes 1572868
  10.6 51.0 %copy-start.2 = (f32[16,2048]{1,0:T(8,128)S(1)}, f32[16,2048]{1,0:T(8,128)}, u32[]{:S(2)}) copy-start(f32[16,2048]{1,0:T(8,128)} %test_ref.1) | copy-start | bytes 393220
  10.6 7.6 %collective-permute-start.2 = (f32[2,8,32,128]{3,2,1,0:T(8,128)S(1)}, f32[2,8,32,128]{3,2,1,0:T(8,128)S(1)}, u32[]{:S(2)}, u32[]{:S(2)}) collective-permute-start(f32[2,8,32,128]{3,2,1,0:T(8,128)S(1)} %get-tuple-element.25), channel_id=1, source_target_pairs={{0,64},{16,80},{64,0},{80,16},{32,96},{48,112},{96,32},{112,48},{1... | collective-permute-start | bytes 786440 | tf_op jit(solution)/shard_map/ppermute | solution.py:170
  14.4 13.1 %collective-permute-start.1 = (f32[8,64,128]{2,1,0:T(8,128)S(1)}, f32[8,64,128]{2,1,0:T(8,128)S(1)}, u32[]{:S(2)}, u32[]{:S(2)}) collective-permute-start(f32[8,64,128]{2,1,0:T(8,128)S(1)} %get-tuple-element.22), channel_id=1, source_target_pairs={{0,16},{16,0},{64,80},{80,64},{32,48},{48,32},{96,112},{112,96},{1... | collective-permute-start | bytes 786440 | tf_op jit(solution)/shard_map/ppermute | solution.py:170
  18.2 9.3 %collective-permute-start.3 = (f32[8,32,128]{2,1,0:T(8,128)S(1)}, f32[8,32,128]{2,1,0:T(8,128)S(1)}, u32[]{:S(2)}, u32[]{:S(2)}) collective-permute-start(f32[8,32,128]{2,1,0:T(8,128)S(1)} %get-tuple-element.27), channel_id=1, source_target_pairs={{0,16},{16,0},{64,80},{80,64},{32,48},{48,32},{96,112},{112,96},{1... | collective-permute-start | bytes 393224 | tf_op jit(solution)/shard_map/ppermute | solution.py:170

commit v8 on v7

--- a/solution.py
+++ b/solution.py
@@ -30,7 +30,7 @@
 
 def place_order(ex_count):
     own = block_place(lax.axis_index("fsdp"))
-    first = 2 - lax.axis_index("ex") % 2
+    first = 1 + lax.axis_index("ex") % 2
     return own ^ first, own ^ 3, own, own ^ 3 ^ first
 
 
@@ -164,7 +164,7 @@
     def swap(value, step):
         pairs = []
         for e in range(ex_count):
-            mask = 2 - e % 2 if step == 0 else 1 + e % 2
+            mask = 1 + e % 2 if step == 0 else 2 - e % 2
             for group in near:
                 pairs += [(f * ex_count + e, group[b ^ mask] * ex_count + e) for b, f in enumerate(group)]
         return lax.ppermute(value, ("fsdp", "ex"), pairs)

time: 81.1 us -> 81.3 us (level)
  transfers between devices with their start and end apart: 4 -> 4, of which waited for: 3 -> 2; matrix products, arithmetic and copies ran while one was open for 0% -> 0% of each run, Pallas kernels for 4% -> 4%
where the time goes in v8:
time: 81.3 us; the launch traced here: 80.9 us
  blocking collectives  51.9 us (64%)
  starting transfers between devices  13.9 us (17%)
  waiting for transfers between devices  7.7 us (9%)
  Pallas kernels  5.77 us (7%)
  local copies, waits for them, and re-layouts  0.88 us (1%)
    all_to_all x1, blocking collectives, shards(): lax.all_to_all(outer, 'fsdp', 0, 0, tiled=True, axis_index_groups=[GATHER...  18.6 us
    all_to_all x1, blocking collectives, shards(): lax.all_to_all(send, 'ex', 0, 0, tiled=True, axis_index_groups=[EX_ORDER])  17.5 us
    all_to_all x1, blocking collectives, shards(): lax.all_to_all(near_sum, 'fsdp', 0, 0, tiled=True, axis_index_groups=[[gr...  15.8 us
    ppermute x4, starting transfers between devices, swap(): return lax.ppermute(value, ('fsdp', 'ex'), pairs)  13.9 us
    ppermute x4, waiting for transfers between devices, swap(): return lax.ppermute(value, ('fsdp', 'ex'), pairs)  7.7 us
    pallas_call x2, Pallas kernels, project_rows(): pl.pallas_call(functools.partial(project_rows_kernel, kept, ex_count), in...  3.62 us
  transfers between devices with their start and end apart: 4, of which 2 were waited for; matrix products, arithmetic and copies ran while one was open for 0% of the time, Pallas kernels for 4%

profile of v8, /device:TPU:1, one launch (start us, length us, event | category | flops | bytes accessed | tf_op | source)
XLA Modules:
  0.0 80.9 jit_solution(4333124909252144055)
XLA Ops:
  0.6 0.0 copy-start
  0.6 0.0 copy-start.3
  0.7 0.9 %copy-done.3 = bf16[128,64]{0,1:T(8,128)(2,1)S(1)} copy-done((bf16[128,64]{0,1:T(8,128)(2,1)S(1)}, bf16[128,64]{0,1:T(8,128)(2,1)}, u32[]{:S(2)}) %copy-start.3) | copy-done | bytes 16408
  1.5 0.0 copy-start.4
  1.5 1.4 %project_in_give.1 = f32[2,8,64,128]{3,2,1,0:T(8,128)S(1)} custom-call(bf16[4096,128]{1,0:T(8,128)(2,1)} %arg_hbm.2, bf16[64,128]{1,0:T(8,128)(2,1)S(1)} %bitcast.6), custom_call_target="tpu_custom_call" | custom-call | tf_op jit(solution)/shard_map/project_in_give/pallas_call | solution.py:184
  2.9 4.0 %collective-permute-start = (f32[2,8,64,128]{3,2,1,0:T(8,128)S(1)}, f32[2,8,64,128]{3,2,1,0:T(8,128)S(1)}, u32[]{:S(2)}, u32[]{:S(2)}) collective-permute-start(f32[2,8,64,128]{3,2,1,0:T(8,128)S(1)} %project_in_give.1), channel_id=1, source_target_pairs={{0,16},{16,0},{64,80},{80,64},{32,48},{48,32},{96,112},{112,96},{1... | collective-permute-start | bytes 1572872 | tf_op jit(solution)/shard_map/ppermute | solution.py:170
  7.0 2.2 %project_in_keep.1.keep_ref = f32[2,8,64,128]{3,2,1,0:T(8,128)} custom-call(bf16[4096,128]{1,0:T(8,128)(2,1)} %arg_hbm.2, bf16[64,128]{1,0:T(8,128)(2,1)} %bitcast.5), custom_call_target="tpu_custom_call" | custom-call | tf_op jit(solution)/shard_map/project_in_keep/pallas_call | solution.py:184
  9.2 0.0 copy-start.1
  9.2 0.0 copy-done
  9.2 0.0 copy-done.4
  9.2 0.6 project_out.1
  9.8 0.0 copy-start.2
  9.8 2.1 %collective-permute-start.2 = (f32[2,8,32,128]{3,2,1,0:T(8,128)S(1)}, f32[2,8,32,128]{3,2,1,0:T(8,128)S(1)}, u32[]{:S(2)}, u32[]{:S(2)}) collective-permute-start(f32[2,8,32,128]{3,2,1,0:T(8,128)S(1)} %get-tuple-element.25), channel_id=1, source_target_pairs={{0,16},{16,0},{64,80},{80,64},{32,48},{48,32},{96,112},{112,96},{1... | collective-permute-start | bytes 786440 | tf_op jit(solution)/shard_map/ppermute | solution.py:170
  11.9 1.6 %collective-permute-done.recv_ref = f32[2,8,64,128]{3,2,1,0:T(8,128)S(1)} collective-permute-done((f32[2,8,64,128]{3,2,1,0:T(8,128)S(1)}, f32[2,8,64,128]{3,2,1,0:T(8,128)S(1)}, u32[]{:S(2)}, u32[]{:S(2)}) %collective-permute-start) | collective-permute-done | bytes 524320 | tf_op jit(solution)/shard_map/ppermute | solution.py:170
  13.5 0.0 copy-done.1
  13.5 0.1 pair_sum.2
  13.6 4.4 %collective-permute-start.1 = (f32[8,64,128]{2,1,0:T(8,128)S(1)}, f32[8,64,128]{2,1,0:T(8,128)S(1)}, u32[]{:S(2)}, u32[]{:S(2)}) collective-permute-start(f32[8,64,128]{2,1,0:T(8,128)S(1)} %get-tuple-element.22), channel_id=1, source_target_pairs={{0,64},{16,80},{64,0},{80,16},{32,96},{48,112},{96,32},{112,48},{1... | collective-permute-start | bytes 786440 | tf_op jit(solution)/shard_map/ppermute | solution.py:170
  18.0 0.0 collective-permute-done.2.recv_ref
  18.1 3.3 %collective-permute-start.3 = (f32[8,32,128]{2,1,0:T(8,128)S(1)}, f32[8,32,128]{2,1,0:T(8,128)S(1)}, u32[]{:S(2)}, u32[]{:S(2)}) collective-permute-start(f32[8,32,128]{2,1,0:T(8,128)S(1)} %get-tuple-element.27), channel_id=1, source_target_pairs={{0,64},{16,80},{64,0},{80,16},{32,96},{48,112},{96,32},{112,48},{1... | collective-permute-start | bytes 393224 | tf_op jit(solution)/shard_map/ppermute | solution.py:170
  21.4 6.1 %collective-permute-done.3.recv_out_ref = f32[8,32,128]{2,1,0:T(8,128)S(1)} collective-permute-done((f32[8,32,128]{2,1,0:T(8,128)S(1)}, f32[8,32,128]{2,1,0:T(8,128)S(1)}, u32[]{:S(2)}, u32[]{:S(2)}) %collective-permute-start.3) | collective-permute-done | bytes 131104 | tf_op jit(solution)/shard_map/ppermute | solution.py:170
  27.5 0.0 collective-permute-done.1.recv_in_ref
  27.6 15.8 %all_to_all.15.parts_ref = f32[8,96,128]{2,1,0:T(8,128)S(1)} all-to-all(f32[8,96,128]{2,1,0:T(8,128)S(1)} %near_sum.1), channel_id=1, replica_groups={{32,384,288,256,416,0,128,160},{48,400,304,272,432,16,144,176},{96,448,..., dimensions={0} | all-to-all | bytes 786432 | tf_op jit(solution)/shard_map/all_to_all | solution.py:228
  43.4 0.3 outer.1
  43.6 18.6 %all_to_all.16.parts_ref = f32[32,16,128]{2,1,0:T(8,128)S(1)} all-to-all(f32[32,16,128]{2,1,0:T(8,128)S(1)} %outer.1), channel_id=1, replica_groups={{144,384,224,160,448,16,80,48,352,336,208,192,368,256,432,96,112,464,12..., dimensions={0} | all-to-all | bytes 524288 | tf_op jit(solution)/shard_map/all_to_all | solution.py:241
  62.2 0.0 copy-done.2
  62.2 0.3 features.1
  62.5 17.5 %all_to_all.17.recv_ref = f32[16,8,128]{2,1,0:T(8,128)S(1)} all-to-all(f32[16,8,128]{2,1,0:T(8,128)S(1)} %get-tuple-element.28), channel_id=1, replica_groups={{10,5,12,9,14,3,0,8,13,2,15,6,11,1,4,7},{26,21,28,25,30,19,16,24,29,18,..., dimensions={0} | all-to-all | bytes 131072 | tf_op jit(solution)/shard_map/all_to_all | solution.py:253
  80.0 0.9 %tile.1 = (f32[64,128]{1,0:T(8,128)}, f32[4,16]{1,0:T(4,128)}) custom-call(f32[16,8,128]{2,1,0:T(8,128)S(1)} %all_to_all.17.recv_ref, f32[4,16]{1,0:T(4,128)S(1)} %get-tuple-element.29.scores_ref), custom_call_target="tpu_custom_call" | custom-call | tf_op jit(solution)/shard_map/tile/pallas_call | solution.py:254
  (2 shorter events, 0.1 us)
Async XLA Ops:
  0.6 8.6 %copy-start = (bf16[4096,344]{0,1:T(8,128)(2,1)S(1)}, bf16[4096,344]{0,1:T(8,128)(2,1)}, u32[]{:S(2)}) copy-start(bf16[4096,344]{0,1:T(8,128)(2,1)} %param.6) | copy-start | bytes 8454148
  0.6 0.9 %copy-start.3 = (bf16[128,64]{0,1:T(8,128)(2,1)S(1)}, bf16[128,64]{0,1:T(8,128)(2,1)}, u32[]{:S(2)}) copy-start(bf16[128,64]{0,1:T(8,128)(2,1)} %param.7) | copy-start | bytes 49156
  1.5 7.7 %copy-start.4 = (bf16[344,32]{0,1:T(8,128)(2,1)S(1)}, bf16[344,32]{0,1:T(8,128)(2,1)}, u32[]{:S(2)}) copy-start(bf16[344,32]{0,1:T(8,128)(2,1)} %param.8) | copy-start | bytes 66052
  2.9 10.6 %collective-permute-start = (f32[2,8,64,128]{3,2,1,0:T(8,128)S(1)}, f32[2,8,64,128]{3,2,1,0:T(8,128)S(1)}, u32[]{:S(2)}, u32[]{:S(2)}) collective-permute-start(f32[2,8,64,128]{3,2,1,0:T(8,128)S(1)} %project_in_give.1), channel_id=1, source_target_pairs={{0,16},{16,0},{64,80},{80,64},{32,48},{48,32},{96,112},{112,96},{1... | collective-permute-start | bytes 1572872 | tf_op jit(solution)/shard_map/ppermute | solution.py:170
  9.2 4.3 %copy-start.1 = (f32[2,8,64,128]{3,2,1,0:T(8,128)S(1)}, f32[2,8,64,128]{3,2,1,0:T(8,128)}, u32[]{:S(2)}) copy-start(f32[2,8,64,128]{3,2,1,0:T(8,128)} %project_in_keep.1.keep_ref) | copy-start | bytes 1572868
  9.8 52.4 %copy-start.2 = (f32[16,2048]{1,0:T(8,128)S(1)}, f32[16,2048]{1,0:T(8,128)}, u32[]{:S(2)}) copy-start(f32[16,2048]{1,0:T(8,128)} %test_ref.1) | copy-start | bytes 393220
  9.8 8.2 %collective-permute-start.2 = (f32[2,8,32,128]{3,2,1,0:T(8,128)S(1)}, f32[2,8,32,128]{3,2,1,0:T(8,128)S(1)}, u32[]{:S(2)}, u32[]{:S(2)}) collective-permute-start(f32[2,8,32,128]{3,2,1,0:T(8,128)S(1)} %get-tuple-element.25), channel_id=1, source_target_pairs={{0,16},{16,0},{64,80},{80,64},{32,48},{48,32},{96,112},{112,96},{1... | collective-permute-start | bytes 786440 | tf_op jit(solution)/shard_map/ppermute | solution.py:170
  13.6 13.9 %collective-permute-start.1 = (f32[8,64,128]{2,1,0:T(8,128)S(1)}, f32[8,64,128]{2,1,0:T(8,128)S(1)}, u32[]{:S(2)}, u32[]{:S(2)}) collective-permute-start(f32[8,64,128]{2,1,0:T(8,128)S(1)} %get-tuple-element.22), channel_id=1, source_target_pairs={{0,64},{16,80},{64,0},{80,16},{32,96},{48,112},{96,32},{112,48},{1... | collective-permute-start | bytes 786440 | tf_op jit(solution)/shard_map/ppermute | solution.py:170
  18.1 9.4 %collective-permute-start.3 = (f32[8,32,128]{2,1,0:T(8,128)S(1)}, f32[8,32,128]{2,1,0:T(8,128)S(1)}, u32[]{:S(2)}, u32[]{:S(2)}) collective-permute-start(f32[8,32,128]{2,1,0:T(8,128)S(1)} %get-tuple-element.27), channel_id=1, source_target_pairs={{0,64},{16,80},{64,0},{80,16},{32,96},{48,112},{96,32},{112,48},{1... | collective-permute-start | bytes 393224 | tf_op jit(solution)/shard_map/ppermute | solution.py:170
